TPU v7x, 768 devices: a whole 4x8x12 slice. The times are simulated.
768 devices in a mesh: down: 192 (over y, z, core), cross: 4 (over x).
Axes of the slice: x: 4, y: 8, z: 12, core: 2. Of those that a mesh axis runs over, the one named last changes fastest.
Arguments:
- right_side: float32 [1536, 128, 256], P('down', 'cross'), may hold values from -6 to 6
- kappa: float32 [1536, 128, 256], P('down', 'cross'), may hold values from 0.3 to 3
- band_mask: int32 [1536, 128, 256], P('down', 'cross'), may hold values 0 or 1
- tile_route: int32 [192, 16], P('down', 'cross'), may hold values from -1 to 7, as said below
Outputs:
- pressure: float32 [1536, 128, 256], P('down', 'cross')
Inputs may be any that keep to these rules, and one draw needn't show every extreme that they name: `tile_route`: within the tiles of one device each value other than -1 occurs at most once; in every draw some owner receives 2 tiles from every device of its cross-slope group.
All inputs are finite; a program needn't handle non-finite values. No bound on the sum of `band_mask` on one device may be relied on, other than what follows from the above.
Results may differ from a plain program's by a relative error of at most 0.0003.
Values sent between devices are 32-bit elements; how exact they have to be, the bound alone decides.
A program may use at most 64 MiB of HBM per device.

v0:
```python
import jax
import jax.numpy as jnp
from jax import lax
from jax.sharding import PartitionSpec as P

TPD = 4
SLOTS = 2
BLOCK_SWEEPS = 4
COARSE_ITERS = 12


OMEGA = 0.8
SNOW_FACTOR = 3.0


def with_halo(block, sides, width):
    for axis, dim in sides:
        count = lax.axis_size(axis)
        forward = [(i, i + 1) for i in range(count - 1)]
        backward = [(target, source) for source, target in forward]
        low = lax.ppermute(
            lax.slice_in_dim(block, block.shape[dim] - width, None, axis=dim), axis, forward
        )
        high = lax.ppermute(lax.slice_in_dim(block, 0, width, axis=dim), axis, backward)
        block = jnp.concatenate([low, block, high], axis=dim)
    return block


def pad_all(field):
    return jnp.pad(field, [(0, 0)] * (field.ndim - 3) + [(1, 1)] * 3)


def pad_vertical(field):
    return jnp.pad(field, ((0, 0), (0, 0), (1, 1)))


def center(padded):
    return padded[..., 1:-1, 1:-1, 1:-1]


def neighbours(padded):
    return [
        padded[..., 2:, 1:-1, 1:-1],
        padded[..., :-2, 1:-1, 1:-1],
        padded[..., 1:-1, 2:, 1:-1],
        padded[..., 1:-1, :-2, 1:-1],
        padded[..., 1:-1, 1:-1, 2:],
        padded[..., 1:-1, 1:-1, :-2],
    ]


def stencil(field_pad, conduct_pad, scale):
    middle = center(field_pad)
    kmiddle = center(conduct_pad)
    total = jnp.zeros_like(middle)
    for other, kother in zip(neighbours(field_pad), neighbours(conduct_pad)):
        total = total + scale * (kmiddle + kother) * (middle - other)
    return total


def diagonal(conduct_pad, scale):
    kmiddle = center(conduct_pad)
    total = jnp.zeros_like(kmiddle)
    for kother in neighbours(conduct_pad):
        total = total + scale * (kmiddle + kother)
    return total


def block_smooth(residual, conduct):
    conduct_pad = pad_all(conduct)
    diag = diagonal(conduct_pad, 2.0)
    safe = jnp.where(diag > 0, diag, 1.0)
    fix = OMEGA * residual / safe
    for sweep in range(BLOCK_SWEEPS - 1):
        fix = fix + OMEGA * (residual - stencil(pad_all(fix), conduct_pad, 2.0)) / safe
    return fix


def coarse_solve(totals, link_down, link_cross, outflow):
    link_up = jnp.concatenate([jnp.zeros_like(link_down[:1]), link_down[:-1]], 0)
    link_back = jnp.concatenate([jnp.zeros_like(link_cross[:, :1]), link_cross[:, :-1]], 1)

    def operate(field):
        padded = jnp.pad(field, 1)
        return (
            outflow * field
            - link_down * padded[2:, 1:-1]
            - link_up * padded[:-2, 1:-1]
            - link_cross * padded[1:-1, 2:]
            - link_back * padded[1:-1, :-2]
        )

    def sweep(step, carry):
        answer, resid, search, norm_now = carry
        image = operate(search)
        alpha = norm_now / jnp.sum(search * image)
        answer = answer + alpha * search
        resid = resid - alpha * image
        norm_next = jnp.sum(resid * resid)
        search = resid + norm_next / norm_now * search
        return (answer, resid, search, norm_next)

    start = (jnp.zeros_like(totals), totals, totals, jnp.sum(totals * totals))
    return lax.fori_loop(0, COARSE_ITERS, sweep, start)[0]


def block_mean(fine):
    rows_here, cols_here, layers = fine.shape
    return (
        fine.reshape(rows_here // 2, 2, cols_here // 2, 2, layers // 2, 2).sum(axis=(1, 3, 5))
        * 0.125
    )


def body(right_side, kappa, band_mask, tile_route):
    conduct = kappa / (1.0 + SNOW_FACTOR * band_mask.astype(jnp.float32))
    rows_here, cols_here, layers = right_side.shape
    half_x, half_y, half_z = (rows_here // 2, cols_here // 2, layers // 2)
    tile_w = half_y // TPD
    conduct_ext = with_halo(conduct, (("down", 0), ("cross", 1)), 2)
    conduct_near = conduct_ext[1:-1, 1:-1]
    near_pad = pad_vertical(conduct_near)
    diag_fine = diagonal(near_pad, 0.5)

    def apply_near(field):
        field_ext = with_halo(field, (("down", 0), ("cross", 1)), 1)
        return stencil(pad_vertical(field_ext), near_pad, 0.5)

    pressure = OMEGA * right_side / diag_fine
    pressure = pressure + OMEGA * (right_side - apply_near(pressure)) / diag_fine
    residual = right_side - apply_near(pressure)
    coarse_res = residual.reshape(half_x, 2, half_y, 2, half_z, 2).sum(axis=(1, 3, 5))
    coarse_con = block_mean(conduct)
    next_down = block_mean(conduct_ext[rows_here + 2 : rows_here + 4, 2:-2])[0]
    prev_down = block_mean(conduct_ext[0:2, 2:-2])[0]
    next_cross = block_mean(conduct_ext[2:-2, cols_here + 2 : cols_here + 4])[:, 0]
    prev_cross = block_mean(conduct_ext[2:-2, 0:2])[:, 0]
    link_down = 2.0 * jnp.sum(coarse_con[-1] + next_down)
    link_up = 2.0 * jnp.sum(coarse_con[0] + prev_down)
    link_cross = 2.0 * jnp.sum(coarse_con[:, -1] + next_cross)
    link_back = 2.0 * jnp.sum(coarse_con[:, 0] + prev_cross)
    vertical = 2.0 * jnp.sum(coarse_con[:, :, 0] + coarse_con[:, :, -1])
    outflow = link_down + link_up + link_cross + link_back + vertical
    totals = jnp.sum(coarse_res)
    summary = jnp.stack([totals, link_down, link_cross, outflow])[None, :]
    tiles_res = coarse_res.reshape(half_x, TPD, tile_w, half_z).transpose(1, 0, 2, 3)
    tiles_con = coarse_con.reshape(half_x, TPD, tile_w, half_z).transpose(1, 0, 2, 3)
    route = tile_route[0]
    n_cross = lax.axis_size("cross")
    onehot = (route[None, :] == jnp.arange(n_cross * SLOTS)[:, None]).astype(jnp.float32)
    send_res = jnp.einsum("st,txyz->sxyz", onehot, tiles_res, precision=lax.Precision.HIGHEST)
    send_con = jnp.einsum("st,txyz->sxyz", onehot, tiles_con, precision=lax.Precision.HIGHEST)
    send_res = send_res.reshape(n_cross, SLOTS, half_x, tile_w, half_z)
    send_con = send_con.reshape(n_cross, SLOTS, half_x, tile_w, half_z)
    fixes = block_smooth(
        lax.all_to_all(send_res, "cross", split_axis=0, concat_axis=0, tiled=True),
        lax.all_to_all(send_con, "cross", split_axis=0, concat_axis=0, tiled=True),
    )
    returned = lax.all_to_all(fixes, "cross", split_axis=0, concat_axis=0, tiled=True)
    returned = returned.reshape(n_cross * SLOTS, half_x, tile_w, half_z)
    tile_fix = jnp.einsum("st,sxyz->txyz", onehot, returned, precision=lax.Precision.HIGHEST)
    tile_fix = tile_fix.transpose(1, 0, 2, 3).reshape(half_x, half_y, half_z)
    n_down = lax.axis_size("down")
    n_cross_all = lax.axis_size("cross")
    table = lax.all_gather(summary, ("down", "cross"), axis=0, tiled=True).reshape(
        n_down, n_cross_all, 4
    )
    answer = coarse_solve(table[:, :, 0], table[:, :, 1], table[:, :, 2], table[:, :, 3])
    brick_fix = lax.dynamic_slice(
        answer, (lax.axis_index("down"), lax.axis_index("cross")), (1, 1)
    )[0, 0]
    correction = tile_fix + brick_fix
    fine_fix = jnp.broadcast_to(
        correction[:, None, :, None, :, None], (half_x, 2, half_y, 2, half_z, 2)
    ).reshape(rows_here, cols_here, layers)
    pressure = pressure + fine_fix
    for sweep in range(2):
        pressure = pressure + OMEGA * (right_side - apply_near(pressure)) / diag_fine
    return pressure


def solution(mesh):
    return jax.shard_map(
        body,
        mesh=mesh,
        in_specs=(
            P("down", "cross", None),
            P("down", "cross", None),
            P("down", "cross", None),
            P("down", "cross"),
        ),
        out_specs=P("down", "cross", None),
        check_vma=False,
    )
```

profile of v0, /device:TPU:32, one launch (start us, length us, event | category | flops | bytes accessed | tf_op | source)
XLA Modules:
  0.0 359.1 jit_solution(4020756510881000241)
XLA Ops:
  1.1 1.9 collective-permute-start.1
  3.0 13.9 %collective-permute-start = (f32[2,32,256]{2,1,0:T(8,128)S(1)}, f32[2,32,256]{2,1,0:T(8,128)S(1)}, u32[]{:S(2)}, u32[]{:S(2)}) collective-permute-start(f32[2,32,256]{2,1,0:T(8,128)S(1)} %get-tuple-element.239), channel_id=1, source_target_pairs={{4,0},{8,4},{12,8},{16,12},{20,16},{24,20},{28,24},{32,28},{36,32}... | collective-permute-start | bytes 196616 | tf_op jit(solution)/shard_map/ppermute | solution.py:24
  17.0 18.1 %reshape.69 = f32[4,2,16,2,128,2]{5,4,3,2,1,0:T(8,128)} reshape(f32[8,32,256]{2,1,0:T(8,128)S(1)} %add_divide_fusion) | data formatting | bytes 524288 | tf_op jit(solution)/shard_map/reshape | solution.py:110
  35.1 7.0 %reduce_sum.170 = f32[4,16,128]{2,1,0:T(8,128)S(1)} reduce(f32[4,2,16,2,128,2]{5,4,3,2,1,0:T(8,128)} %reshape.69, f32[]{:T(128)} %constant.23.clone.1), dimensions={1,3,5}, to_apply=%region_1.2 | reduce | flops 57344 | bytes 294916 | tf_op jit(solution)/shard_map/reduce_sum | solution.py:110
  43.1 4.3 %all-to-all-start.1 = ((f32[4,2,4,4,128]{4,1,3,2,0:T(2,128)}), f32[4,2,4,4,128]{4,1,3,2,0:T(2,128)S(1)}, u32[]{:S(2)}, u32[]{:S(2)}) async-start(f32[4,2,4,4,128]{4,1,3,2,0:T(2,128)} %copy.29), calls=%async_computation.1 | async-start | bytes 131072 | tf_op jit(solution)/shard_map/all_to_all | solution.py:157
  48.7 3.9 %collective-permute-start.3 = (f32[12,2,256]{2,1,0:T(2,128)S(1)}, f32[12,2,256]{2,1,0:T(2,128)S(1)}, u32[]{:S(2)}, u32[]{:S(2)}) collective-permute-start(f32[12,2,256]{2,1,0:T(2,128)S(1)} %get-tuple-element.220), channel_id=1, source_target_pairs={{0,1},{1,2},{2,3},{4,5},{5,6},{6,7},{8,9},{9,10},{10,11},{12,13},{... | collective-permute-start | bytes 73736 | tf_op jit(solution)/shard_map/ppermute | solution.py:21
  54.0 2.1 reduce_sum.173
  56.4 2.1 reduce_sum.181
  61.6 1.9 collective-permute-start.5
  63.5 7.0 %collective-permute-start.4 = (f32[1,32,256]{2,1,0:T(8,128)S(1)}, f32[1,32,256]{2,1,0:T(8,128)S(1)}, u32[]{:S(2)}, u32[]{:S(2)}) collective-permute-start(f32[1,32,256]{2,1,0:T(8,128)S(1)} %get-tuple-element.237), channel_id=1, source_target_pairs={{4,0},{8,4},{12,8},{16,12},{20,16},{24,20},{28,24},{32,28},{36,32}... | collective-permute-start | bytes 98312 | tf_op jit(solution)/shard_map/ppermute | solution.py:24
  72.1 4.5 %collective-permute-start.7 = (f32[10,1,256]{2,1,0:T(1,128)S(1)}, f32[10,1,256]{2,1,0:T(1,128)S(1)}, u32[]{:S(2)}, u32[]{:S(2)}) collective-permute-start(f32[10,1,256]{2,1,0:T(1,128)S(1)} %get-tuple-element.228), channel_id=1, source_target_pairs={{0,1},{1,2},{2,3},{4,5},{5,6},{6,7},{8,9},{9,10},{10,11},{12,13},{... | collective-permute-start | bytes 30728 | tf_op jit(solution)/shard_map/ppermute | solution.py:21
  78.6 3.6 %collective-permute-done.6 = f32[10,1,256]{2,1,0:T(1,128)S(1)} collective-permute-done((f32[10,1,256]{2,1,0:T(1,128)S(1)}, f32[10,1,256]{2,1,0:T(1,128)S(1)}, u32[]{:S(2)}, u32[]{:S(2)}) %collective-permute-start.6) | collective-permute-done | bytes 10272 | tf_op jit(solution)/shard_map/ppermute | solution.py:24
  82.9 1.9 collective-permute-start.9
  84.8 7.0 %collective-permute-start.8 = (f32[1,32,256]{2,1,0:T(8,128)S(1)}, f32[1,32,256]{2,1,0:T(8,128)S(1)}, u32[]{:S(2)}, u32[]{:S(2)}) collective-permute-start(f32[1,32,256]{2,1,0:T(8,128)S(1)} %get-tuple-element.235), channel_id=1, source_target_pairs={{4,0},{8,4},{12,8},{16,12},{20,16},{24,20},{28,24},{32,28},{36,32}... | collective-permute-start | bytes 98312 | tf_op jit(solution)/shard_map/ppermute | solution.py:24
  93.4 3.4 collective-permute-start.11
  100.2 2.1 collective-permute-done.10
  103.5 18.1 %reshape.66 = f32[4,2,16,2,128,2]{5,4,3,2,1,0:T(8,128)} reshape(f32[8,32,256]{2,1,0:T(8,128)S(1)} %get-tuple-element.201) | data formatting | bytes 524288 | tf_op jit(solution)/shard_map/reshape | solution.py:132
  121.6 7.0 %reduce_sum.169 = f32[4,16,128]{2,1,0:T(8,128)S(1)} reduce(f32[4,2,16,2,128,2]{5,4,3,2,1,0:T(8,128)} %reshape.66, f32[]{:T(128)} %constant.23.clone.1), dimensions={1,3,5}, to_apply=%region_0.1 | reduce | flops 57344 | bytes 294916 | tf_op jit(solution)/shard_map/reduce_sum | solution.py:132
  129.5 107.0 %all-reduce.12 = f32[3072]{0:T(1024)S(1)} all-reduce(f32[3072]{0:T(1024)S(1)} %maximum_dynamic-update-slice_fusion), channel_id=2, replica_groups=mesh['down'=192,'cross'=4] {'down','cross'}, use_global_device_ids=true, to_apply=%add.12 | all-reduce | flops 3072 | bytes 24576
  240.5 3.3 all-to-all-start
  251.2 3.8 %all-to-all-start.2 = ((f32[4,2,4,4,128]{4,1,3,2,0:T(2,128)}), f32[4,2,4,4,128]{4,1,3,2,0:T(2,128)S(1)}, u32[]{:S(2)}, u32[]{:S(2)}) async-start(f32[4,2,4,4,128]{4,1,3,2,0:T(2,128)} %divide_add_fusion), calls=%async_computation.2 | async-start | bytes 131072 | tf_op jit(solution)/shard_map/all_to_all | solution.py:159
  255.0 41.8 %while.19 = (s32[]{:T(128)}, f32[192,4]{0,1:T(4,128)S(1)}, f32[192,4]{0,1:T(4,128)S(1)}, f32[192,4]{0,1:T(4,128)S(1)}, f32[]{:T(128)}, /*index=5*/f32[192,4]{0,1...) while((s32[]{:T(128)}, f32[192,4]{0,1:T(4,128)S(1)}, ...), condition=%wide.region_20.21_spmd.clone, body=%wide.region_17.20_spmd.clone.sunk | while | flops 15363 | bytes 46259 | solution.py:104
  298.4 6.3 %broadcast_in_dim.21 = f32[4,2,16,2,128,2]{5,4,3,2,1,0:T(8,128)} broadcast(f32[4,16,128]{2,1,0:T(8,128)S(1)} %bitcast.62), dimensions={0,2,4} | broadcast | bytes 294912 | tf_op jit(solution)/shard_map/broadcast_in_dim | solution.py:173
  304.8 12.7 %reshape.73 = f32[8,32,256]{2,1,0:T(8,128)S(1)} reshape(f32[4,2,16,2,128,2]{5,4,3,2,1,0:T(8,128)} %broadcast_in_dim.21) | data formatting | bytes 524288 | tf_op jit(solution)/shard_map/reshape | solution.py:175
  317.5 1.9 collective-permute-start.13
  319.5 7.0 %collective-permute-start.12 = (f32[1,32,256]{2,1,0:T(8,128)S(1)}, f32[1,32,256]{2,1,0:T(8,128)S(1)}, u32[]{:S(2)}, u32[]{:S(2)}) collective-permute-start(f32[1,32,256]{2,1,0:T(8,128)S(1)} %get-tuple-element.233), channel_id=1, source_target_pairs={{4,0},{8,4},{12,8},{16,12},{20,16},{24,20},{28,24},{32,28},{36,32}... | collective-permute-start | bytes 98312 | tf_op jit(solution)/shard_map/ppermute | solution.py:24
  328.0 3.9 %collective-permute-start.15 = (f32[10,1,256]{2,1,0:T(1,128)S(1)}, f32[10,1,256]{2,1,0:T(1,128)S(1)}, u32[]{:S(2)}, u32[]{:S(2)}) collective-permute-start(f32[10,1,256]{2,1,0:T(1,128)S(1)} %get-tuple-element.224), channel_id=1, source_target_pairs={{0,1},{1,2},{2,3},{4,5},{5,6},{6,7},{8,9},{9,10},{10,11},{12,13},{... | collective-permute-start | bytes 30728 | tf_op jit(solution)/shard_map/ppermute | solution.py:21
  333.3 4.2 %collective-permute-done.14 = f32[10,1,256]{2,1,0:T(1,128)S(1)} collective-permute-done((f32[10,1,256]{2,1,0:T(1,128)S(1)}, f32[10,1,256]{2,1,0:T(1,128)S(1)}, u32[]{:S(2)}, u32[]{:S(2)}) %collective-permute-start.14) | collective-permute-done | bytes 10272 | tf_op jit(solution)/shard_map/ppermute | solution.py:24
  338.2 1.9 collective-permute-start.17
  340.2 7.0 %collective-permute-start.16 = (f32[1,32,256]{2,1,0:T(8,128)S(1)}, f32[1,32,256]{2,1,0:T(8,128)S(1)}, u32[]{:S(2)}, u32[]{:S(2)}) collective-permute-start(f32[1,32,256]{2,1,0:T(8,128)S(1)} %get-tuple-element.231), channel_id=1, source_target_pairs={{4,0},{8,4},{12,8},{16,12},{20,16},{24,20},{28,24},{32,28},{36,32}... | collective-permute-start | bytes 98312 | tf_op jit(solution)/shard_map/ppermute | solution.py:24
  348.7 3.4 collective-permute-start.19
  353.5 4.2 %collective-permute-done.18 = f32[10,1,256]{2,1,0:T(1,128)S(1)} collective-permute-done((f32[10,1,256]{2,1,0:T(1,128)S(1)}, f32[10,1,256]{2,1,0:T(1,128)S(1)}, u32[]{:S(2)}, u32[]{:S(2)}) %collective-permute-start.18) | collective-permute-done | bytes 10272 | tf_op jit(solution)/shard_map/ppermute | solution.py:24
  (129 shorter events, 54.5 us)
Async XLA Ops:
  1.1 47.6 %collective-permute-start.1 = (f32[2,32,256]{2,1,0:T(8,128)S(1)}, f32[2,32,256]{2,1,0:T(8,128)S(1)}, u32[]{:S(2)}, u32[]{:S(2)}) collective-permute-start(f32[2,32,256]{2,1,0:T(8,128)S(1)} %get-tuple-element.238), channel_id=1, source_target_pairs={{0,4},{4,8},{8,12},{12,16},{16,20},{20,24},{24,28},{28,32},{32,36}... | collective-permute-start | bytes 196616 | tf_op jit(solution)/shard_map/ppermute | solution.py:21
  3.0 39.1 %copy-start.1 = (s32[1,4]{1,0:T(1,128)S(1)}, s32[1,4]{1,0:T(1,128)}, u32[]{:S(2)}) copy-start(s32[1,4]{1,0:T(1,128)} %param.9) | copy-start | bytes 52
  3.0 45.7 %collective-permute-start = (f32[2,32,256]{2,1,0:T(8,128)S(1)}, f32[2,32,256]{2,1,0:T(8,128)S(1)}, u32[]{:S(2)}, u32[]{:S(2)}) collective-permute-start(f32[2,32,256]{2,1,0:T(8,128)S(1)} %get-tuple-element.239), channel_id=1, source_target_pairs={{4,0},{8,4},{12,8},{16,12},{20,16},{24,20},{28,24},{32,28},{36,32}... | collective-permute-start | bytes 196616 | tf_op jit(solution)/shard_map/ppermute | solution.py:24
  35.1 26.2 %copy-start = (f32[8,32,256]{2,1,0:T(8,128)S(1)}, f32[8,32,256]{2,1,0:T(8,128)}, u32[]{:S(2)}) copy-start(f32[8,32,256]{2,1,0:T(8,128)} %param.6) | copy-start | bytes 786436
  43.1 197.5 %all-to-all-start.1 = ((f32[4,2,4,4,128]{4,1,3,2,0:T(2,128)}), f32[4,2,4,4,128]{4,1,3,2,0:T(2,128)S(1)}, u32[]{:S(2)}, u32[]{:S(2)}) async-start(f32[4,2,4,4,128]{4,1,3,2,0:T(2,128)} %copy.29), calls=%async_computation.1 | async-start | bytes 131072 | tf_op jit(solution)/shard_map/all_to_all | solution.py:157
  48.7 12.2 %collective-permute-start.3 = (f32[12,2,256]{2,1,0:T(2,128)S(1)}, f32[12,2,256]{2,1,0:T(2,128)S(1)}, u32[]{:S(2)}, u32[]{:S(2)}) collective-permute-start(f32[12,2,256]{2,1,0:T(2,128)S(1)} %get-tuple-element.220), channel_id=1, source_target_pairs={{0,1},{1,2},{2,3},{4,5},{5,6},{6,7},{8,9},{9,10},{10,11},{12,13},{... | collective-permute-start | bytes 73736 | tf_op jit(solution)/shard_map/ppermute | solution.py:21
  52.7 8.3 %collective-permute-start.2 = (f32[12,2,256]{2,1,0:T(2,128)S(1)}, f32[12,2,256]{2,1,0:T(2,128)S(1)}, u32[]{:S(2)}, u32[]{:S(2)}) collective-permute-start(f32[12,2,256]{2,1,0:T(2,128)S(1)} %get-tuple-element.221), channel_id=1, source_target_pairs={{1,0},{2,1},{3,2},{5,4},{6,5},{7,6},{9,8},{10,9},{11,10},{13,12},{... | collective-permute-start | bytes 73736 | tf_op jit(solution)/shard_map/ppermute | solution.py:24
  61.6 8.9 %collective-permute-start.5 = (f32[1,32,256]{2,1,0:T(8,128)S(1)}, f32[1,32,256]{2,1,0:T(8,128)S(1)}, u32[]{:S(2)}, u32[]{:S(2)}) collective-permute-start(f32[1,32,256]{2,1,0:T(8,128)S(1)} %get-tuple-element.236), channel_id=1, source_target_pairs={{0,4},{4,8},{8,12},{12,16},{16,20},{20,24},{24,28},{28,32},{32,36}... | collective-permute-start | bytes 98312 | tf_op jit(solution)/shard_map/ppermute | solution.py:21
  63.5 8.5 %collective-permute-start.4 = (f32[1,32,256]{2,1,0:T(8,128)S(1)}, f32[1,32,256]{2,1,0:T(8,128)S(1)}, u32[]{:S(2)}, u32[]{:S(2)}) collective-permute-start(f32[1,32,256]{2,1,0:T(8,128)S(1)} %get-tuple-element.237), channel_id=1, source_target_pairs={{4,0},{8,4},{12,8},{16,12},{20,16},{24,20},{28,24},{32,28},{36,32}... | collective-permute-start | bytes 98312 | tf_op jit(solution)/shard_map/ppermute | solution.py:24
  72.1 6.5 %collective-permute-start.7 = (f32[10,1,256]{2,1,0:T(1,128)S(1)}, f32[10,1,256]{2,1,0:T(1,128)S(1)}, u32[]{:S(2)}, u32[]{:S(2)}) collective-permute-start(f32[10,1,256]{2,1,0:T(1,128)S(1)} %get-tuple-element.228), channel_id=1, source_target_pairs={{0,1},{1,2},{2,3},{4,5},{5,6},{6,7},{8,9},{9,10},{10,11},{12,13},{... | collective-permute-start | bytes 30728 | tf_op jit(solution)/shard_map/ppermute | solution.py:21
  76.6 5.6 %collective-permute-start.6 = (f32[10,1,256]{2,1,0:T(1,128)S(1)}, f32[10,1,256]{2,1,0:T(1,128)S(1)}, u32[]{:S(2)}, u32[]{:S(2)}) collective-permute-start(f32[10,1,256]{2,1,0:T(1,128)S(1)} %get-tuple-element.229), channel_id=1, source_target_pairs={{1,0},{2,1},{3,2},{5,4},{6,5},{7,6},{9,8},{10,9},{11,10},{13,12},{... | collective-permute-start | bytes 30728 | tf_op jit(solution)/shard_map/ppermute | solution.py:24
  82.9 10.2 %collective-permute-start.9 = (f32[1,32,256]{2,1,0:T(8,128)S(1)}, f32[1,32,256]{2,1,0:T(8,128)S(1)}, u32[]{:S(2)}, u32[]{:S(2)}) collective-permute-start(f32[1,32,256]{2,1,0:T(8,128)S(1)} %get-tuple-element.234), channel_id=1, source_target_pairs={{0,4},{4,8},{8,12},{12,16},{16,20},{20,24},{24,28},{28,32},{32,36}... | collective-permute-start | bytes 98312 | tf_op jit(solution)/shard_map/ppermute | solution.py:21
  84.8 8.5 %collective-permute-start.8 = (f32[1,32,256]{2,1,0:T(8,128)S(1)}, f32[1,32,256]{2,1,0:T(8,128)S(1)}, u32[]{:S(2)}, u32[]{:S(2)}) collective-permute-start(f32[1,32,256]{2,1,0:T(8,128)S(1)} %get-tuple-element.235), channel_id=1, source_target_pairs={{4,0},{8,4},{12,8},{16,12},{20,16},{24,20},{28,24},{32,28},{36,32}... | collective-permute-start | bytes 98312 | tf_op jit(solution)/shard_map/ppermute | solution.py:24
  93.4 6.8 %collective-permute-start.11 = (f32[10,1,256]{2,1,0:T(1,128)S(1)}, f32[10,1,256]{2,1,0:T(1,128)S(1)}, u32[]{:S(2)}, u32[]{:S(2)}) collective-permute-start(f32[10,1,256]{2,1,0:T(1,128)S(1)} %get-tuple-element.226), channel_id=1, source_target_pairs={{0,1},{1,2},{2,3},{4,5},{5,6},{6,7},{8,9},{9,10},{10,11},{12,13},{... | collective-permute-start | bytes 30728 | tf_op jit(solution)/shard_map/ppermute | solution.py:21
  96.7 5.6 %collective-permute-start.10 = (f32[10,1,256]{2,1,0:T(1,128)S(1)}, f32[10,1,256]{2,1,0:T(1,128)S(1)}, u32[]{:S(2)}, u32[]{:S(2)}) collective-permute-start(f32[10,1,256]{2,1,0:T(1,128)S(1)} %get-tuple-element.227), channel_id=1, source_target_pairs={{1,0},{2,1},{3,2},{5,4},{6,5},{7,6},{9,8},{10,9},{11,10},{13,12},{... | collective-permute-start | bytes 30728 | tf_op jit(solution)/shard_map/ppermute | solution.py:24
  240.5 8.9 %all-to-all-start = ((f32[4,2,4,4,128]{4,1,3,2,0:T(2,128)}), f32[4,2,4,4,128]{4,1,3,2,0:T(2,128)S(1)}, u32[]{:S(2)}, u32[]{:S(2)}) async-start(f32[4,2,4,4,128]{4,1,3,2,0:T(2,128)} %copy.27), calls=%async_computation | async-start | bytes 131072 | tf_op jit(solution)/shard_map/all_to_all | solution.py:156
  251.2 46.2 %all-to-all-start.2 = ((f32[4,2,4,4,128]{4,1,3,2,0:T(2,128)}), f32[4,2,4,4,128]{4,1,3,2,0:T(2,128)S(1)}, u32[]{:S(2)}, u32[]{:S(2)}) async-start(f32[4,2,4,4,128]{4,1,3,2,0:T(2,128)} %divide_add_fusion), calls=%async_computation.2 | async-start | bytes 131072 | tf_op jit(solution)/shard_map/all_to_all | solution.py:159
  317.5 8.9 %collective-permute-start.13 = (f32[1,32,256]{2,1,0:T(8,128)S(1)}, f32[1,32,256]{2,1,0:T(8,128)S(1)}, u32[]{:S(2)}, u32[]{:S(2)}) collective-permute-start(f32[1,32,256]{2,1,0:T(8,128)S(1)} %get-tuple-element.232), channel_id=1, source_target_pairs={{0,4},{4,8},{8,12},{12,16},{16,20},{20,24},{24,28},{28,32},{32,36}... | collective-permute-start | bytes 98312 | tf_op jit(solution)/shard_map/ppermute | solution.py:21
  319.5 8.5 %collective-permute-start.12 = (f32[1,32,256]{2,1,0:T(8,128)S(1)}, f32[1,32,256]{2,1,0:T(8,128)S(1)}, u32[]{:S(2)}, u32[]{:S(2)}) collective-permute-start(f32[1,32,256]{2,1,0:T(8,128)S(1)} %get-tuple-element.233), channel_id=1, source_target_pairs={{4,0},{8,4},{12,8},{16,12},{20,16},{24,20},{28,24},{32,28},{36,32}... | collective-permute-start | bytes 98312 | tf_op jit(solution)/shard_map/ppermute | solution.py:24
  328.0 5.3 %collective-permute-start.15 = (f32[10,1,256]{2,1,0:T(1,128)S(1)}, f32[10,1,256]{2,1,0:T(1,128)S(1)}, u32[]{:S(2)}, u32[]{:S(2)}) collective-permute-start(f32[10,1,256]{2,1,0:T(1,128)S(1)} %get-tuple-element.224), channel_id=1, source_target_pairs={{0,1},{1,2},{2,3},{4,5},{5,6},{6,7},{8,9},{9,10},{10,11},{12,13},{... | collective-permute-start | bytes 30728 | tf_op jit(solution)/shard_map/ppermute | solution.py:21
  332.0 5.6 %collective-permute-start.14 = (f32[10,1,256]{2,1,0:T(1,128)S(1)}, f32[10,1,256]{2,1,0:T(1,128)S(1)}, u32[]{:S(2)}, u32[]{:S(2)}) collective-permute-start(f32[10,1,256]{2,1,0:T(1,128)S(1)} %get-tuple-element.225), channel_id=1, source_target_pairs={{1,0},{2,1},{3,2},{5,4},{6,5},{7,6},{9,8},{10,9},{11,10},{13,12},{... | collective-permute-start | bytes 30728 | tf_op jit(solution)/shard_map/ppermute | solution.py:24
  338.2 8.9 %collective-permute-start.17 = (f32[1,32,256]{2,1,0:T(8,128)S(1)}, f32[1,32,256]{2,1,0:T(8,128)S(1)}, u32[]{:S(2)}, u32[]{:S(2)}) collective-permute-start(f32[1,32,256]{2,1,0:T(8,128)S(1)} %get-tuple-element.230), channel_id=1, source_target_pairs={{0,4},{4,8},{8,12},{12,16},{16,20},{20,24},{24,28},{28,32},{32,36}... | collective-permute-start | bytes 98312 | tf_op jit(solution)/shard_map/ppermute | solution.py:21
  340.2 8.5 %collective-permute-start.16 = (f32[1,32,256]{2,1,0:T(8,128)S(1)}, f32[1,32,256]{2,1,0:T(8,128)S(1)}, u32[]{:S(2)}, u32[]{:S(2)}) collective-permute-start(f32[1,32,256]{2,1,0:T(8,128)S(1)} %get-tuple-element.231), channel_id=1, source_target_pairs={{4,0},{8,4},{12,8},{16,12},{20,16},{24,20},{28,24},{32,28},{36,32}... | collective-permute-start | bytes 98312 | tf_op jit(solution)/shard_map/ppermute | solution.py:24
  348.7 4.7 %collective-permute-start.19 = (f32[10,1,256]{2,1,0:T(1,128)S(1)}, f32[10,1,256]{2,1,0:T(1,128)S(1)}, u32[]{:S(2)}, u32[]{:S(2)}) collective-permute-start(f32[10,1,256]{2,1,0:T(1,128)S(1)} %get-tuple-element.222), channel_id=1, source_target_pairs={{0,1},{1,2},{2,3},{4,5},{5,6},{6,7},{8,9},{9,10},{10,11},{12,13},{... | collective-permute-start | bytes 30728 | tf_op jit(solution)/shard_map/ppermute | solution.py:21
  352.1 5.6 %collective-permute-start.18 = (f32[10,1,256]{2,1,0:T(1,128)S(1)}, f32[10,1,256]{2,1,0:T(1,128)S(1)}, u32[]{:S(2)}, u32[]{:S(2)}) collective-permute-start(f32[10,1,256]{2,1,0:T(1,128)S(1)} %get-tuple-element.223), channel_id=1, source_target_pairs={{1,0},{2,1},{3,2},{5,4},{6,5},{7,6},{9,8},{10,9},{11,10},{13,12},{... | collective-permute-start | bytes 30728 | tf_op jit(solution)/shard_map/ppermute | solution.py:24
where the time goes:
time: 361 us; the launch traced here: 359 us
  blocking collectives  107 us (30%)
  starting transfers between devices  88.5 us (25%)
  local copies, waits for them, and re-layouts  69.4 us (19%)
  other arithmetic  44.2 us (12%)
  loops' own time  24.4 us (7%)
  waiting for transfers between devices  20.3 us (6%)
  between operations  3.92 us (1%)
    unnamed x1, blocking collectives  107 us
    ppermute x10, starting transfers between devices, with_halo(): lax.ppermute(lax.slice_in_dim(block, 0, width, axis=dim), axis, backward)  48.4 us
    ppermute x10, starting transfers between devices, with_halo(): lax.ppermute(lax.slice_in_dim(block, block.shape[dim] - width, None, axis...  28.7 us
    another operation x1, loops' own time, coarse_solve(): return lax.fori_loop(0, COARSE_ITERS, sweep, start)[0]  24.4 us
    ppermute x10, waiting for transfers between devices, with_halo(): lax.ppermute(lax.slice_in_dim(block, 0, width, axis=dim), axis, backward)  19.1 us
    reshape x1, local copies, waits for them, and re-layouts, block_mean(): fine.reshape(rows_here // 2, 2, cols_here // 2, 2, layers // 2, 2)  18.1 us
    reshape x1, local copies, waits for them, and re-layouts, body(): residual.reshape(half_x, 2, half_y, 2, half_z, 2).sum(axis=(1, 3, 5))  18.1 us
    reshape x1, local copies, waits for them, and re-layouts, body(): fine_fix = jnp.broadcast_to(correction[:, None, :, None, :, None], (half_...  12.7 us
  transfers between devices with their start and end apart: 23, of which 11 were waited for; matrix products, arithmetic and copies ran while one was open for 25% of the time, Pallas kernels for 0%

commit v1 on v0

v1 whole, which is shorter than its diff:
```python
import jax
import jax.numpy as jnp
from jax import lax
from jax.experimental import pallas as pl
from jax.experimental.pallas import tpu as pltpu
from jax.sharding import PartitionSpec as P

OMEGA = 0.8
BLOCK_SWEEPS = 4
COARSE_ITERS = 12
CHIPS_Z = 12

MESH = pl.DeviceIdType.MESH
CORNERS = ((-1, -1), (-1, 1), (1, -1), (1, 1))
F32 = jnp.float32


def iota(shape, dim):
    return lax.broadcasted_iota(jnp.int32, shape, dim)


def flag(cond):
    return jnp.where(cond, 1.0, 0.0).astype(F32)


def total_of(value):
    return jnp.sum(jnp.sum(value, axis=0, keepdims=True), axis=1, keepdims=True)


def side_sum(value):
    rows, lanes = value.shape
    lane = iota(value.shape, 1)
    return (
        pltpu.roll(value, 1, 0)
        + pltpu.roll(value, rows - 1, 0)
        + jnp.where(lane > 0, pltpu.roll(value, 1, 1), 0.0)
        + jnp.where(lane < lanes - 1, pltpu.roll(value, lanes - 1, 1), 0.0)
    )


def tile_side_sum(value):
    rows, lanes = value.shape
    lane = iota(value.shape, 1)
    row = iota(value.shape, 0) % 8
    return (
        jnp.where(row >= 2, pltpu.roll(value, 2, 0), 0.0)
        + jnp.where(row < 6, pltpu.roll(value, rows - 2, 0), 0.0)
        + jnp.where(lane >= 2, pltpu.roll(value, 2, 1), 0.0)
        + jnp.where(lane < lanes - 2, pltpu.roll(value, lanes - 2, 1), 0.0)
    )


def pair_sum(value):
    rows, lanes = value.shape
    row, lane = iota(value.shape, 0), iota(value.shape, 1)
    value = value + jnp.where(row % 2 == 0, pltpu.roll(value, rows - 1, 0), pltpu.roll(value, 1, 0))
    return value + jnp.where(
        lane % 2 == 0, pltpu.roll(value, lanes - 1, 1), pltpu.roll(value, 1, 1)
    )


def make_kernel(n_down, n_cross, nz):
    ny = n_down // (2 * nz)
    half = nz // 2

    def kernel(
        rhs_hbm, kappa_hbm, mask_hbm, route, out,
        E, R, MK, D, W, PA, PB, Q, RES, CR, CC, WT, FA, FB,
        SX, LX, LK, M1, G1, M2, G2, M3, G3,
        load_sem, h_send, h_recv, q_send, q_recv,
        s1, r1, s2, r2, s3, r3,
    ):
        d = lax.axis_index("down")
        c = lax.axis_index("cross")
        core = lax.rem(d, 2)
        chip = lax.div(d, 2)
        z = lax.rem(chip, nz)
        y = lax.div(chip, nz)

        loads = [
            pltpu.make_async_copy(kappa_hbm, E.at[3:11, 8:40, :], load_sem.at[0]),
            pltpu.make_async_copy(mask_hbm, MK, load_sem.at[1]),
            pltpu.make_async_copy(rhs_hbm, R.at[3:11, 8:40, :], load_sem.at[2]),
        ]
        for load in loads:
            load.start()

        d_next, d_prev = lax.rem(d + 1, n_down), lax.rem(d + n_down - 1, n_down)
        c_next, c_prev = lax.rem(c + 1, n_cross), lax.rem(c + n_cross - 1, n_cross)
        near = [(d_prev, c), (d_next, c), (d, c_prev), (d, c_next)]
        corners = [
            (d_prev if sx < 0 else d_next, c_prev if sy < 0 else c_next) for sx, sy in CORNERS
        ]
        n1 = 2 * n_cross
        me1 = c * 2 + core
        group1 = []
        for k in range(1, n1):
            g = lax.rem(me1 + k, n1)
            group1.append((chip * 2 + lax.rem(g, 2), lax.div(g, 2)))
        group2 = [((lax.rem(y + k, ny) * nz + z) * 2 + core, c) for k in range(1, ny)]
        group3 = [((y * nz + lax.rem(z + k, nz)) * 2 + core, c) for k in range(1, nz)]

        barrier = pltpu.get_barrier_semaphore()
        peers = near + corners + group1 + group2 + group3
        for peer in peers:
            pl.semaphore_signal(barrier, inc=1, device_id=peer, device_id_type=MESH)

        m_up, m_dn = flag(d > 0), flag(d < n_down - 1)
        m_l, m_r = flag(c > 0), flag(c < n_cross - 1)

        zero8 = jnp.zeros((8, 256), F32)
        for i in (0, 13):
            E[i, 0:8, :] = zero8
            E[i, 40:48, :] = zero8
        loads[0].wait()
        loads[1].wait()

        @pl.loop(0, 8)
        def _(x):
            kap = E[x + 3, 8:40, :]
            E[x + 3, 8:40, :] = jnp.where(MK[x] > 0, kap * 0.25, kap)

        loads[2].wait()
        sub8 = iota((8, 256), 0)

        @pl.loop(0, 8)
        def _(x):
            SX[0, x] = jnp.where(sub8 < 3, E[x + 3, 8:16, :], pltpu.roll(R[x + 3, 8:16, :], 3, 0))
            SX[1, x] = jnp.where(sub8 >= 5, E[x + 3, 32:40, :], pltpu.roll(R[x + 3, 32:40, :], 5, 0))

        pl.semaphore_wait(barrier, len(peers))

        def remote(src, dst, send, recv, k, peer):
            return pltpu.make_async_remote_copy(
                src_ref=src, dst_ref=dst, send_sem=send.at[k], recv_sem=recv.at[k],
                device_id=peer, device_id_type=MESH,
            )

        halo = [
            remote(E.at[3:6, 8:40, :], E.at[11:14, 8:40, :], h_send, h_recv, 0, near[0]),
            remote(E.at[8:11, 8:40, :], E.at[0:3, 8:40, :], h_send, h_recv, 1, near[1]),
            remote(SX.at[0], LX.at[1], h_send, h_recv, 2, near[2]),
            remote(SX.at[1], LX.at[0], h_send, h_recv, 3, near[3]),
            remote(R.at[3:5, 8:40, :], R.at[11:13, 8:40, :], h_send, h_recv, 4, near[0]),
            remote(R.at[9:11, 8:40, :], R.at[1:3, 8:40, :], h_send, h_recv, 5, near[1]),
        ]
        for k, (sx, sy) in enumerate(CORNERS):
            rows = slice(0, 2) if sx < 0 else slice(6, 8)
            src = SX.at[0 if sy < 0 else 1, rows]
            halo.append(remote(src, LK.at[3 - k], h_send, h_recv, 6 + k, corners[k]))
        for k in (6, 7, 8, 9, 0, 1, 2, 3, 4, 5):
            halo[k].start()
        for copy in halo:
            copy.wait_recv()

        def unpack(tile, i, left, keep):
            if left:
                E[i, 0:8, :] = jnp.where(sub8 >= 5, tile, 0.0) * keep
                R[i, 0:8, :] = jnp.where(sub8 >= 6, pltpu.roll(tile, 3, 0), 0.0) * keep
            else:
                E[i, 40:48, :] = jnp.where(sub8 < 3, tile, 0.0) * keep
                R[i, 40:48, :] = jnp.where(sub8 < 2, pltpu.roll(tile, 5, 0), 0.0) * keep

        @pl.loop(0, 8)
        def _(x):
            unpack(LX[0, x], x + 3, True, m_l)
            unpack(LX[1, x], x + 3, False, m_r)

        @pl.loop(0, 2)
        def _(x):
            unpack(LK[0, x], x + 1, True, m_l * m_up)
            unpack(LK[1, x], x + 1, False, m_r * m_up)
            unpack(LK[2, x], x + 11, True, m_l * m_dn)
            unpack(LK[3, x], x + 11, False, m_r * m_dn)
            R[x + 1, 8:40, :] = R[x + 1, 8:40, :] * m_up
            R[x + 11, 8:40, :] = R[x + 11, 8:40, :] * m_dn

        @pl.loop(0, 3)
        def _(x):
            E[x, 8:40, :] = E[x, 8:40, :] * m_up
            E[x + 11, 8:40, :] = E[x + 11, 8:40, :] * m_dn

        @pl.loop(1, 13)
        def _(i):
            q = E[i]
            diag = 3.0 * q + 0.5 * (E[i - 1] + E[i + 1] + side_sum(q))
            inside = q > 0
            w = jnp.where(inside, OMEGA / jnp.where(inside, diag, 1.0), 0.0)
            D[i] = diag
            W[i] = w
            PA[i] = w * R[i]

        def coupling(p, i):
            q, v = E[i], p[i]
            around = p[i - 1] + p[i + 1] + side_sum(v)
            return 0.5 * (q * around + E[i - 1] * p[i - 1] + E[i + 1] * p[i + 1] + side_sum(q * v))

        def relax(p, i):
            return (1.0 - OMEGA) * p[i] + W[i] * (R[i] + coupling(p, i))

        @pl.loop(2, 12)
        def _(i):
            PB[i] = relax(PA, i)

        def residual_row(x, carry):
            acc, con = carry
            i = x + 3
            res = (R[i] - D[i] * PB[i] + coupling(PB, i))[8:40]
            RES[x] = res
            return acc + res, con + E[i]

        acc, con = lax.fori_loop(
            0, 8, residual_row, (jnp.zeros((32, 256), F32), jnp.zeros((48, 256), F32))
        )

        sub48, lane48 = iota((48, 256), 0), iota((48, 256), 1)
        own = (sub48 >= 8) & (sub48 < 40)
        down = E[9] + E[10] + E[11] + E[12]
        up = E[1] + E[2] + E[3] + E[4]
        cross = jnp.where((sub48 >= 38) & (sub48 < 42), con, 0.0)
        back = jnp.where((sub48 >= 6) & (sub48 < 10), con, 0.0)
        ends = jnp.where(own & ((lane48 < 2) | (lane48 >= 254)), con, 0.0)
        down = jnp.where(own, down, 0.0)
        outflow = 0.25 * total_of(down + jnp.where(own, up, 0.0) + cross + back + ends)
        sums = [total_of(acc), outflow, 0.25 * total_of(down), 0.25 * total_of(cross)]
        my_lane = lax.rem(z, 2) * 64 + y * 8 + me1
        here = iota((1, 128), 1) == my_lane
        for k, value in enumerate(sums):
            M1[k : k + 1, :] = jnp.where(here, value, 0.0)

        gather1 = [remote(M1, G1.at[k], s1, r1, k, group1[k]) for k in range(n1 - 1)]
        gather2 = [remote(M2, G2.at[k], s2, r2, k, group2[k]) for k in range(ny - 1)]
        gather3 = [remote(M3, G3.at[k], s3, r3, k, group3[k]) for k in range(nz - 1)]
        for copy in gather1:
            copy.start()

        zero32 = jnp.zeros((32, 256), F32)
        for ref in (CC, FA, FB):
            ref[0] = zero32
            ref[5] = zero32

        @pl.loop(0, 4)
        def _(x):
            CR[x] = pair_sum(RES[2 * x] + RES[2 * x + 1])
            CC[x + 1] = 0.125 * pair_sum(E[2 * x + 3, 8:40, :] + E[2 * x + 4, 8:40, :])

        @pl.loop(1, 5)
        def _(i):
            q = CC[i]
            wt = OMEGA / (2.0 * (6.0 * q + CC[i - 1] + CC[i + 1] + tile_side_sum(q)))
            WT[i - 1] = wt
            FA[i] = wt * CR[i - 1]

        def tile_relax(f, i):
            q, v = CC[i], f[i]
            around = f[i - 1] + f[i + 1] + tile_side_sum(v)
            more = CC[i - 1] * f[i - 1] + CC[i + 1] * f[i + 1] + tile_side_sum(q * v)
            return (1.0 - OMEGA) * v + WT[i - 1] * (CR[i - 1] + 2.0 * (q * around + more))

        f, g = FA, FB
        for sweep in range(BLOCK_SWEEPS - 1):

            @pl.loop(1, 5)
            def _(i, f=f, g=g):
                g[i] = tile_relax(f, i)

            f, g = g, f

        tile_of_row = iota((32, 256), 0) // 8
        cloud = jnp.zeros((32, 256), F32)
        for t in range(4):
            cloud = jnp.where(tile_of_row == t, flag(route[0, t] >= 0), cloud)

        @pl.loop(0, 4)
        def _(x):
            fix = f[x + 1] * cloud
            Q[2 * x + 3, 8:40, :] = PB[2 * x + 3, 8:40, :] + fix
            Q[2 * x + 4, 8:40, :] = PB[2 * x + 4, 8:40, :] + fix

        for copy in gather1:
            copy.wait_recv()
        row = M1[...]
        for k in range(n1 - 1):
            row = row + G1[k]
        M2[...] = row
        for copy in gather2:
            copy.start()

        src_rows = {-1: slice(3, 5), 1: slice(9, 11)}
        dst_rows = {-1: slice(11, 13), 1: slice(1, 3)}
        src_cols = {-1: slice(8, 16), 1: slice(32, 40)}
        dst_cols = {-1: slice(40, 48), 1: slice(0, 8)}
        mid, band = slice(3, 11), slice(8, 40)
        fix_halo = []
        for k, sx in enumerate((-1, 1)):
            src, dst = Q.at[src_rows[sx], band, :], Q.at[dst_rows[sx], band, :]
            fix_halo.append(remote(src, dst, q_send, q_recv, k, near[k]))
        for k, sy in enumerate((-1, 1)):
            src, dst = Q.at[mid, src_cols[sy], :], Q.at[mid, dst_cols[sy], :]
            fix_halo.append(remote(src, dst, q_send, q_recv, 2 + k, near[2 + k]))
        for k, (sx, sy) in enumerate(CORNERS):
            src = Q.at[src_rows[sx], src_cols[sy], :]
            dst = Q.at[dst_rows[sx], dst_cols[sy], :]
            fix_halo.append(remote(src, dst, q_send, q_recv, 4 + k, corners[k]))
        for copy in fix_halo:
            copy.start()

        for copy in gather2:
            copy.wait_recv()
        row = M2[...]
        for k in range(ny - 1):
            row = row + G2[k]
        M3[...] = row
        for copy in gather3:
            copy.start()
        for copy in fix_halo:
            copy.wait_recv()

        sub, lane = iota((8, 128), 0), iota((8, 128), 1)
        tz = 2 * sub + lane // 64
        ty = (lane % 64) // 8
        tc = (lane % 8) // 2
        odd = lane % 2 == 1

        for copy in gather3:
            copy.wait_recv()
        table = [jnp.where(sub == lax.div(z, 2), M3[k : k + 1, :], 0.0) for k in range(4)]
        for j in range(nz - 1):
            from_z = lax.rem(z + nz - 1 - j, nz)
            at = sub == lax.div(from_z, 2)
            for k in range(4):
                table[k] = table[k] + jnp.where(at, G3[j, k : k + 1, :], 0.0)
        totals, outs, link_dn, link_cr = table

        def ahead(value, by):
            return pltpu.roll(value, (-by) % 128, 1)

        def shift_rows(value, by):
            return pltpu.roll(value, by % 8, 0)

        def next_parts(value):
            v63 = ahead(value, 63)
            return ahead(value, 1), v63, shift_rows(v63, -1), shift_rows(ahead(value, 71), half - 1)

        def prev_parts(value):
            v63 = ahead(value, -63)
            return (
                ahead(value, -1), v63, shift_rows(v63, 1), shift_rows(ahead(value, -71), 1 - half)
            )

        last = (ty == ny - 1) & (tz == nz - 1)
        first = (ty == 0) & (tz == 0)
        next_at = (
            ~odd,
            odd & (tz % 2 == 0),
            odd & (tz % 2 == 1) & (tz < nz - 1),
            odd & (tz == nz - 1) & ~last,
        )
        prev_at = (
            odd,
            ~odd & (tz % 2 == 1),
            ~odd & (tz % 2 == 0) & (tz > 0),
            ~odd & (tz == 0) & ~first,
        )
        link_up = jnp.zeros((8, 128), F32)
        held = (tz < nz) & (ty < ny) & (tc < n_cross)
        for at, part in zip(prev_at, prev_parts(link_dn)):
            link_up = jnp.where(at & held, part, link_up)
        link_bk = jnp.where((tc > 0) & held, ahead(link_cr, -2), 0.0)
        link_cr = jnp.where(tc < n_cross - 1, link_cr, 0.0)
        next_w = [jnp.where(at, link_dn, 0.0) for at in next_at]
        prev_w = [jnp.where(at, link_up, 0.0) for at in prev_at]

        def operate(value):
            image = outs * value - link_cr * ahead(value, 2) - link_bk * ahead(value, -2)
            for weight, part in zip(next_w, next_parts(value)):
                image = image - weight * part
            for weight, part in zip(prev_w, prev_parts(value)):
                image = image - weight * part
            return image

        def iterate(step, carry):
            answer, resid, search, norm_now = carry
            image = operate(search)
            alpha = norm_now / total_of(search * image)
            answer = answer + alpha * search
            resid = resid - alpha * image
            norm_next = total_of(resid * resid)
            search = resid + norm_next / norm_now * search
            return answer, resid, search, norm_next

        start = (jnp.zeros((8, 128), F32), totals, totals, total_of(totals * totals))
        answer = lax.fori_loop(0, COARSE_ITERS, iterate, start)[0]

        def brick(dd, cc):
            core_b, chip_b = lax.rem(dd, 2), lax.div(dd, 2)
            z_b, y_b = lax.rem(chip_b, nz), lax.div(chip_b, nz)
            at_lane = lax.rem(z_b, 2) * 64 + y_b * 8 + cc * 2 + core_b
            return total_of(jnp.where((sub == lax.div(z_b, 2)) & (lane == at_lane), answer, 0.0))

        col = iota((48, 256), 0)
        keep_col = jnp.where(col < 8, m_l, jnp.where(col < 40, 1.0, m_r))

        def brick_row(dd):
            left, mine, right = brick(dd, c_prev), brick(dd, c), brick(dd, c_next)
            return jnp.where(col < 8, left, jnp.where(col < 40, mine, right))

        for dd, lo, hi, keep in ((d_prev, 1, 3, m_up), (d, 3, 11, None), (d_next, 11, 13, m_dn)):
            add = brick_row(dd)
            mask = keep_col if keep is None else keep_col * keep

            @pl.loop(lo, hi)
            def _(i, add=add, mask=mask):
                PA[i] = (Q[i] + add) * mask

        @pl.loop(2, 12)
        def _(i):
            PB[i] = relax(PA, i)

        @pl.loop(3, 11)
        def _(i):
            out[i - 3] = relax(PB, i)[8:40]

        for copy in halo + gather1 + gather2 + gather3 + fix_halo:
            copy.wait_send()

    return kernel


def solution(mesh):
    n_down, n_cross = mesh.shape["down"], mesh.shape["cross"]
    nz = CHIPS_Z
    ny = n_down // (2 * nz)
    n1 = 2 * n_cross
    big = pltpu.VMEM((14, 48, 256), F32)
    dma = pltpu.SemaphoreType.DMA
    msg = pltpu.VMEM((4, 128), F32)

    def body(right_side, kappa, band_mask, tile_route):
        return pl.pallas_call(
            make_kernel(n_down, n_cross, nz),
            out_shape=jax.ShapeDtypeStruct(right_side.shape, F32),
            in_specs=[pl.BlockSpec(memory_space=pl.ANY)] * 3
            + [pl.BlockSpec(memory_space=pltpu.SMEM)],
            out_specs=pl.BlockSpec(memory_space=pltpu.VMEM),
            scratch_shapes=[
                big, big, pltpu.VMEM((8, 32, 256), jnp.int32), big, big, big, big, big,
                pltpu.VMEM((8, 32, 256), F32),
                pltpu.VMEM((4, 32, 256), F32), pltpu.VMEM((6, 32, 256), F32),
                pltpu.VMEM((4, 32, 256), F32), pltpu.VMEM((6, 32, 256), F32),
                pltpu.VMEM((6, 32, 256), F32),
                pltpu.VMEM((2, 8, 8, 256), F32), pltpu.VMEM((2, 8, 8, 256), F32),
                pltpu.VMEM((4, 2, 8, 256), F32),
                msg, pltpu.VMEM((n1 - 1, 4, 128), F32),
                msg, pltpu.VMEM((ny - 1, 4, 128), F32),
                msg, pltpu.VMEM((nz - 1, 4, 128), F32),
                dma((3,)), dma((10,)), dma((10,)), dma((8,)), dma((8,)),
                dma((n1 - 1,)), dma((n1 - 1,)), dma((ny - 1,)), dma((ny - 1,)),
                dma((nz - 1,)), dma((nz - 1,)),
            ],
            compiler_params=pltpu.CompilerParams(collective_id=0, has_side_effects=True),
            name="cycle",
        )(right_side, kappa, band_mask, tile_route)

    return jax.shard_map(
        body,
        mesh=mesh,
        in_specs=(
            P("down", "cross", None),
            P("down", "cross", None),
            P("down", "cross", None),
            P("down", "cross"),
        ),
        out_specs=P("down", "cross", None),
        check_vma=False,
    )
```

time: 361 us -> 50.8 us (0.14)
  the two profiles are of different devices: /device:TPU:32 before, /device:TPU:1 now
where the time goes in v1:
time: 50.8 us; the launch traced here: 50.6 us
  Pallas kernels  48.9 us (96%)
  local copies, waits for them, and re-layouts  1.67 us (3%)
    pallas_call x1, Pallas kernels, body(): pl.pallas_call(make_kernel(n_down, n_cross, nz), out_shape=jax.ShapeDtype...  48.9 us
    unnamed x1, local copies, waits for them, and re-layouts  1.67 us

profile of v1, /device:TPU:1, one launch (start us, length us, event | category | flops | bytes accessed | tf_op | source)
XLA Modules:
  0.0 50.6 jit_solution(11986516427175984998)
XLA Ops:
  0.0 48.9 %cycle.1 = f32[8,32,256]{2,1,0:T(8,128)} custom-call(f32[8,32,256]{2,1,0:T(8,128)} %rhs_hbm.1, f32[8,32,256]{2,1,0:T(8,128)} %kappa_hbm.1, s32[8,32,256]{2,1,0:T(8,128)} %mask_hbm.1, s32[1,4]{1,0:T(1,128)} %route.1), custom_call_target="tpu_custom_call" | custom-call | tf_op jit(solution)/shard_map/cycle/pallas_call | solution.py:440
  48.9 1.7 %copy.6 = f32[8,32,256]{2,1,0:T(8,128)} copy(f32[8,32,256]{2,1,0:T(8,128)} %cycle.1) | data formatting | bytes 524288

commit v2 on v1

--- a/solution.py
+++ b/solution.py
@@ -27,26 +27,25 @@
     return jnp.sum(jnp.sum(value, axis=0, keepdims=True), axis=1, keepdims=True)
 
 
-def side_sum(value):
+def shifted(value, by, tile=0):
     rows, lanes = value.shape
-    lane = iota(value.shape, 1)
+    row, lane = iota(value.shape, 0) % max(tile, 1), iota(value.shape, 1)
+    back, ahead = pltpu.roll(value, by, 0), pltpu.roll(value, rows - by, 0)
+    if tile:
+        back = jnp.where(row >= by, back, 0.0)
+        ahead = jnp.where(row < tile - by, ahead, 0.0)
+    below = jnp.where(lane >= by, pltpu.roll(value, by, 1), 0.0)
+    above = jnp.where(lane < lanes - by, pltpu.roll(value, lanes - by, 1), 0.0)
+    return back, ahead, below, above
+
+
+def rolled(value, by, rows_out):
+    rows, lanes = value.shape
     return (
-        pltpu.roll(value, 1, 0)
-        + pltpu.roll(value, rows - 1, 0)
-        + jnp.where(lane > 0, pltpu.roll(value, 1, 1), 0.0)
-        + jnp.where(lane < lanes - 1, pltpu.roll(value, lanes - 1, 1), 0.0)
-    )
-
-
-def tile_side_sum(value):
-    rows, lanes = value.shape
-    lane = iota(value.shape, 1)
-    row = iota(value.shape, 0) % 8
-    return (
-        jnp.where(row >= 2, pltpu.roll(value, 2, 0), 0.0)
-        + jnp.where(row < 6, pltpu.roll(value, rows - 2, 0), 0.0)
-        + jnp.where(lane >= 2, pltpu.roll(value, 2, 1), 0.0)
-        + jnp.where(lane < lanes - 2, pltpu.roll(value, lanes - 2, 1), 0.0)
+        pltpu.roll(value, by, 0)[:rows_out],
+        pltpu.roll(value, rows - by, 0)[:rows_out],
+        pltpu.roll(value[:rows_out], by, 1),
+        pltpu.roll(value[:rows_out], lanes - by, 1),
     )
 
 
@@ -65,8 +64,8 @@
 
     def kernel(
         rhs_hbm, kappa_hbm, mask_hbm, route, out,
-        E, R, MK, D, W, PA, PB, Q, RES, CR, CC, WT, FA, FB,
-        SX, LX, LK, M1, G1, M2, G2, M3, G3,
+        E, R, MK, D, W, PA, PB, Q, FX, FY, FZ, RES, CR, CC, WT, TX, TY, TZ, FA, FB,
+        SX, LX, LK, QX, QK, M1, G1, M2, G2, M3, G3,
         load_sem, h_send, h_recv, q_send, q_recv,
         s1, r1, s2, r2, s3, r3,
     ):
@@ -78,9 +77,9 @@
         y = lax.div(chip, nz)
 
         loads = [
-            pltpu.make_async_copy(kappa_hbm, E.at[3:11, 8:40, :], load_sem.at[0]),
+            pltpu.make_async_copy(kappa_hbm, E.at[3:11, 0:32, :], load_sem.at[0]),
             pltpu.make_async_copy(mask_hbm, MK, load_sem.at[1]),
-            pltpu.make_async_copy(rhs_hbm, R.at[3:11, 8:40, :], load_sem.at[2]),
+            pltpu.make_async_copy(rhs_hbm, R.at[3:11, 0:32, :], load_sem.at[2]),
         ]
         for load in loads:
             load.start()
@@ -110,23 +109,22 @@
 
         zero8 = jnp.zeros((8, 256), F32)
         for i in (0, 13):
-            E[i, 0:8, :] = zero8
-            E[i, 40:48, :] = zero8
+            E[i, 32:40, :] = zero8
         loads[0].wait()
         loads[1].wait()
 
         @pl.loop(0, 8)
         def _(x):
-            kap = E[x + 3, 8:40, :]
-            E[x + 3, 8:40, :] = jnp.where(MK[x] > 0, kap * 0.25, kap)
+            kap = E[x + 3, 0:32, :]
+            E[x + 3, 0:32, :] = jnp.where(MK[x] > 0, kap * 0.25, kap)
 
         loads[2].wait()
         sub8 = iota((8, 256), 0)
 
         @pl.loop(0, 8)
         def _(x):
-            SX[0, x] = jnp.where(sub8 < 3, E[x + 3, 8:16, :], pltpu.roll(R[x + 3, 8:16, :], 3, 0))
-            SX[1, x] = jnp.where(sub8 >= 5, E[x + 3, 32:40, :], pltpu.roll(R[x + 3, 32:40, :], 5, 0))
+            SX[0, x] = jnp.where(sub8 < 3, E[x + 3, 0:8, :], pltpu.roll(R[x + 3, 0:8, :], 3, 0))
+            SX[1, x] = jnp.where(sub8 >= 5, E[x + 3, 24:32, :], pltpu.roll(R[x + 3, 24:32, :], 5, 0))
 
         pl.semaphore_wait(barrier, len(peers))
 
@@ -137,12 +135,12 @@
             )
 
         halo = [
-            remote(E.at[3:6, 8:40, :], E.at[11:14, 8:40, :], h_send, h_recv, 0, near[0]),
-            remote(E.at[8:11, 8:40, :], E.at[0:3, 8:40, :], h_send, h_recv, 1, near[1]),
+            remote(E.at[3:6, 0:32, :], E.at[11:14, 0:32, :], h_send, h_recv, 0, near[0]),
+            remote(E.at[8:11, 0:32, :], E.at[0:3, 0:32, :], h_send, h_recv, 1, near[1]),
             remote(SX.at[0], LX.at[1], h_send, h_recv, 2, near[2]),
             remote(SX.at[1], LX.at[0], h_send, h_recv, 3, near[3]),
-            remote(R.at[3:5, 8:40, :], R.at[11:13, 8:40, :], h_send, h_recv, 4, near[0]),
-            remote(R.at[9:11, 8:40, :], R.at[1:3, 8:40, :], h_send, h_recv, 5, near[1]),
+            remote(R.at[3:5, 0:32, :], R.at[11:13, 0:32, :], h_send, h_recv, 4, near[0]),
+            remote(R.at[9:11, 0:32, :], R.at[1:3, 0:32, :], h_send, h_recv, 5, near[1]),
         ]
         for k, (sx, sy) in enumerate(CORNERS):
             rows = slice(0, 2) if sx < 0 else slice(6, 8)
@@ -153,73 +151,79 @@
         for copy in halo:
             copy.wait_recv()
 
-        def unpack(tile, i, left, keep):
-            if left:
-                E[i, 0:8, :] = jnp.where(sub8 >= 5, tile, 0.0) * keep
-                R[i, 0:8, :] = jnp.where(sub8 >= 6, pltpu.roll(tile, 3, 0), 0.0) * keep
-            else:
-                E[i, 40:48, :] = jnp.where(sub8 < 3, tile, 0.0) * keep
-                R[i, 40:48, :] = jnp.where(sub8 < 2, pltpu.roll(tile, 5, 0), 0.0) * keep
+        def unpack(left, right, i, keep):
+            right, left = right * (m_r * keep), left * (m_l * keep)
+            E[i, 32:40, :] = jnp.where(sub8 < 3, right, jnp.where(sub8 >= 5, left, 0.0))
+            right, left = pltpu.roll(right, 5, 0), pltpu.roll(left, 3, 0)
+            R[i, 32:40, :] = jnp.where(sub8 < 2, right, jnp.where(sub8 >= 6, left, 0.0))
 
         @pl.loop(0, 8)
         def _(x):
-            unpack(LX[0, x], x + 3, True, m_l)
-            unpack(LX[1, x], x + 3, False, m_r)
+            unpack(LX[0, x], LX[1, x], x + 3, 1.0)
 
         @pl.loop(0, 2)
         def _(x):
-            unpack(LK[0, x], x + 1, True, m_l * m_up)
-            unpack(LK[1, x], x + 1, False, m_r * m_up)
-            unpack(LK[2, x], x + 11, True, m_l * m_dn)
-            unpack(LK[3, x], x + 11, False, m_r * m_dn)
-            R[x + 1, 8:40, :] = R[x + 1, 8:40, :] * m_up
-            R[x + 11, 8:40, :] = R[x + 11, 8:40, :] * m_dn
+            unpack(LK[0, x], LK[1, x], x + 1, m_up)
+            unpack(LK[2, x], LK[3, x], x + 11, m_dn)
+            R[x + 1, 0:32, :] = R[x + 1, 0:32, :] * m_up
+            R[x + 11, 0:32, :] = R[x + 11, 0:32, :] * m_dn
 
         @pl.loop(0, 3)
         def _(x):
-            E[x, 8:40, :] = E[x, 8:40, :] * m_up
-            E[x + 11, 8:40, :] = E[x + 11, 8:40, :] * m_dn
+            E[x, 0:32, :] = E[x, 0:32, :] * m_up
+            E[x + 11, 0:32, :] = E[x + 11, 0:32, :] * m_dn
+
+        lane40 = iota((40, 256), 1)
 
         @pl.loop(1, 13)
         def _(i):
             q = E[i]
-            diag = 3.0 * q + 0.5 * (E[i - 1] + E[i + 1] + side_sum(q))
+            back, ahead_, below, above = shifted(q, 1)
+            up, dn = E[i - 1], E[i + 1]
+            diag = 3.0 * q + 0.5 * (((up + dn) + (back + ahead_)) + (below + above))
             inside = q > 0
             w = jnp.where(inside, OMEGA / jnp.where(inside, diag, 1.0), 0.0)
+            FX[i] = 0.5 * (up + q)
+            FX[i + 1] = 0.5 * (dn + q)
+            FY[0, i] = 0.5 * (back + q)
+            FY[1, i] = 0.5 * (ahead_ + q)
+            FZ[0, i] = jnp.where(lane40 > 0, 0.5 * (below + q), 0.0)
+            FZ[1, i] = jnp.where(lane40 < 255, 0.5 * (above + q), 0.0)
             D[i] = diag
             W[i] = w
             PA[i] = w * R[i]
 
-        def coupling(p, i):
-            q, v = E[i], p[i]
-            around = p[i - 1] + p[i + 1] + side_sum(v)
-            return 0.5 * (q * around + E[i - 1] * p[i - 1] + E[i + 1] * p[i + 1] + side_sum(q * v))
-
-        def relax(p, i):
-            return (1.0 - OMEGA) * p[i] + W[i] * (R[i] + coupling(p, i))
+        def coupling(p, i, n):
+            back, ahead_, below, above = rolled(p[i], 1, n)
+            along = FX[i, :n] * p[i - 1, :n] + FX[i + 1, :n] * p[i + 1, :n]
+            across = FY[0, i, :n] * back + FY[1, i, :n] * ahead_
+            return (along + across) + (FZ[0, i, :n] * below + FZ[1, i, :n] * above)
+
+        def relax(p, i, n):
+            return (1.0 - OMEGA) * p[i, :n] + W[i, :n] * (R[i, :n] + coupling(p, i, n))
 
         @pl.loop(2, 12)
         def _(i):
-            PB[i] = relax(PA, i)
+            PB[i] = relax(PA, i, 40)
 
         def residual_row(x, carry):
             acc, con = carry
             i = x + 3
-            res = (R[i] - D[i] * PB[i] + coupling(PB, i))[8:40]
+            res = R[i, :32] - D[i, :32] * PB[i, :32] + coupling(PB, i, 32)
             RES[x] = res
             return acc + res, con + E[i]
 
         acc, con = lax.fori_loop(
-            0, 8, residual_row, (jnp.zeros((32, 256), F32), jnp.zeros((48, 256), F32))
+            0, 8, residual_row, (jnp.zeros((32, 256), F32), jnp.zeros((40, 256), F32))
         )
 
-        sub48, lane48 = iota((48, 256), 0), iota((48, 256), 1)
-        own = (sub48 >= 8) & (sub48 < 40)
+        sub40 = iota((40, 256), 0)
+        own = sub40 < 32
         down = E[9] + E[10] + E[11] + E[12]
         up = E[1] + E[2] + E[3] + E[4]
-        cross = jnp.where((sub48 >= 38) & (sub48 < 42), con, 0.0)
-        back = jnp.where((sub48 >= 6) & (sub48 < 10), con, 0.0)
-        ends = jnp.where(own & ((lane48 < 2) | (lane48 >= 254)), con, 0.0)
+        cross = jnp.where((sub40 >= 30) & (sub40 < 34), con, 0.0)
+        back = jnp.where((sub40 < 2) | (sub40 >= 38), con, 0.0)
+        ends = jnp.where(own & ((lane40 < 2) | (lane40 >= 254)), con, 0.0)
         down = jnp.where(own, down, 0.0)
         outflow = 0.25 * total_of(down + jnp.where(own, up, 0.0) + cross + back + ends)
         sums = [total_of(acc), outflow, 0.25 * total_of(down), 0.25 * total_of(cross)]
@@ -242,20 +246,33 @@
         @pl.loop(0, 4)
         def _(x):
             CR[x] = pair_sum(RES[2 * x] + RES[2 * x + 1])
-            CC[x + 1] = 0.125 * pair_sum(E[2 * x + 3, 8:40, :] + E[2 * x + 4, 8:40, :])
+            CC[x + 1] = 0.125 * pair_sum(E[2 * x + 3, 0:32, :] + E[2 * x + 4, 0:32, :])
+
+        lane32, row32 = iota((32, 256), 1), iota((32, 256), 0) % 8
 
         @pl.loop(1, 5)
         def _(i):
             q = CC[i]
-            wt = OMEGA / (2.0 * (6.0 * q + CC[i - 1] + CC[i + 1] + tile_side_sum(q)))
-            WT[i - 1] = wt
+            back, ahead_, below, above = shifted(q, 2, 8)
+            up, dn = CC[i - 1], CC[i + 1]
+            diag = 12.0 * q + 2.0 * (((up + dn) + (back + ahead_)) + (below + above))
+            wt = OMEGA / diag
+            TX[i] = 2.0 * (up + q)
+            TX[i + 1] = 2.0 * (dn + q)
+            TY[0, i] = jnp.where(row32 >= 2, 2.0 * (back + q), 0.0)
+            TY[1, i] = jnp.where(row32 < 6, 2.0 * (ahead_ + q), 0.0)
+            TZ[0, i] = jnp.where(lane32 >= 2, 2.0 * (below + q), 0.0)
+            TZ[1, i] = jnp.where(lane32 < 254, 2.0 * (above + q), 0.0)
+            WT[i] = wt
             FA[i] = wt * CR[i - 1]
 
         def tile_relax(f, i):
-            q, v = CC[i], f[i]
-            around = f[i - 1] + f[i + 1] + tile_side_sum(v)
-            more = CC[i - 1] * f[i - 1] + CC[i + 1] * f[i + 1] + tile_side_sum(q * v)
-            return (1.0 - OMEGA) * v + WT[i - 1] * (CR[i - 1] + 2.0 * (q * around + more))
+            v = f[i]
+            back, ahead_, below, above = rolled(v, 2, 32)
+            along = TX[i] * f[i - 1] + TX[i + 1] * f[i + 1]
+            across = TY[0, i] * back + TY[1, i] * ahead_
+            around = (along + across) + (TZ[0, i] * below + TZ[1, i] * above)
+            return (1.0 - OMEGA) * v + WT[i] * (CR[i - 1] + around)
 
         f, g = FA, FB
         for sweep in range(BLOCK_SWEEPS - 1):
@@ -274,8 +291,8 @@
         @pl.loop(0, 4)
         def _(x):
             fix = f[x + 1] * cloud
-            Q[2 * x + 3, 8:40, :] = PB[2 * x + 3, 8:40, :] + fix
-            Q[2 * x + 4, 8:40, :] = PB[2 * x + 4, 8:40, :] + fix
+            Q[2 * x + 3, 0:32, :] = PB[2 * x + 3, 0:32, :] + fix
+            Q[2 * x + 4, 0:32, :] = PB[2 * x + 4, 0:32, :] + fix
 
         for copy in gather1:
             copy.wait_recv()
@@ -288,20 +305,18 @@
 
         src_rows = {-1: slice(3, 5), 1: slice(9, 11)}
         dst_rows = {-1: slice(11, 13), 1: slice(1, 3)}
-        src_cols = {-1: slice(8, 16), 1: slice(32, 40)}
-        dst_cols = {-1: slice(40, 48), 1: slice(0, 8)}
-        mid, band = slice(3, 11), slice(8, 40)
+        src_cols = {-1: slice(0, 8), 1: slice(24, 32)}
+        mid, band = slice(3, 11), slice(0, 32)
         fix_halo = []
         for k, sx in enumerate((-1, 1)):
             src, dst = Q.at[src_rows[sx], band, :], Q.at[dst_rows[sx], band, :]
             fix_halo.append(remote(src, dst, q_send, q_recv, k, near[k]))
         for k, sy in enumerate((-1, 1)):
-            src, dst = Q.at[mid, src_cols[sy], :], Q.at[mid, dst_cols[sy], :]
-            fix_halo.append(remote(src, dst, q_send, q_recv, 2 + k, near[2 + k]))
+            src = Q.at[mid, src_cols[sy], :]
+            fix_halo.append(remote(src, QX.at[1 - k], q_send, q_recv, 2 + k, near[2 + k]))
         for k, (sx, sy) in enumerate(CORNERS):
-            src = Q.at[src_rows[sx], src_cols[sy], :]
-            dst = Q.at[dst_rows[sx], dst_cols[sy], :]
-            fix_halo.append(remote(src, dst, q_send, q_recv, 4 + k, corners[k]))
+            src = Q.at[3 if sx < 0 else 10, src_cols[sy], :]
+            fix_halo.append(remote(src, QK.at[3 - k], q_send, q_recv, 4 + k, corners[k]))
         for copy in fix_halo:
             copy.start()
 
@@ -398,28 +413,37 @@
             at_lane = lax.rem(z_b, 2) * 64 + y_b * 8 + cc * 2 + core_b
             return total_of(jnp.where((sub == lax.div(z_b, 2)) & (lane == at_lane), answer, 0.0))
 
-        col = iota((48, 256), 0)
-        keep_col = jnp.where(col < 8, m_l, jnp.where(col < 40, 1.0, m_r))
-
-        def brick_row(dd):
-            left, mine, right = brick(dd, c_prev), brick(dd, c), brick(dd, c_next)
-            return jnp.where(col < 8, left, jnp.where(col < 40, mine, right))
-
-        for dd, lo, hi, keep in ((d_prev, 1, 3, m_up), (d, 3, 11, None), (d_next, 11, 13, m_dn)):
-            add = brick_row(dd)
-            mask = keep_col if keep is None else keep_col * keep
+        for dd, lo, hi, keep in ((d_prev, 1, 3, m_up), (d, 3, 11, 1.0), (d_next, 11, 13, m_dn)):
+            left, own_, right = brick(dd, c_prev), brick(dd, c), brick(dd, c_next)
 
             @pl.loop(lo, hi)
-            def _(i, add=add, mask=mask):
-                PA[i] = (Q[i] + add) * mask
+            def _(i, own_=own_, keep=keep):
+                PA[i, 0:32, :] = (Q[i, 0:32, :] + own_) * keep
+
+            def beside(side_l, side_r, left=left, right=right, keep=keep):
+                tile = jnp.where(sub8 < 4, (side_r + right) * m_r, (side_l + left) * m_l)
+                return tile * keep
+
+            if lo == 3:
+
+                @pl.loop(0, 8)
+                def _(x, beside=beside):
+                    PA[x + 3, 32:40, :] = beside(QX[0, x], QX[1, x])
+
+            elif lo == 1:
+                PA[1, 32:40, :] = zero8
+                PA[2, 32:40, :] = beside(QK[0], QK[1])
+            else:
+                PA[11, 32:40, :] = beside(QK[2], QK[3])
+                PA[12, 32:40, :] = zero8
 
         @pl.loop(2, 12)
         def _(i):
-            PB[i] = relax(PA, i)
+            PB[i] = relax(PA, i, 40)
 
         @pl.loop(3, 11)
         def _(i):
-            out[i - 3] = relax(PB, i)[8:40]
+            out[i - 3] = relax(PB, i, 32)
 
         for copy in halo + gather1 + gather2 + gather3 + fix_halo:
             copy.wait_send()
@@ -432,25 +456,29 @@
     nz = CHIPS_Z
     ny = n_down // (2 * nz)
     n1 = 2 * n_cross
-    big = pltpu.VMEM((14, 48, 256), F32)
+    big = pltpu.VMEM((14, 40, 256), F32)
+    two = pltpu.VMEM((2, 14, 40, 256), F32)
+    coarse = pltpu.VMEM((6, 32, 256), F32)
+    coarse2 = pltpu.VMEM((2, 6, 32, 256), F32)
     dma = pltpu.SemaphoreType.DMA
     msg = pltpu.VMEM((4, 128), F32)
 
     def body(right_side, kappa, band_mask, tile_route):
         return pl.pallas_call(
             make_kernel(n_down, n_cross, nz),
-            out_shape=jax.ShapeDtypeStruct(right_side.shape, F32),
+            out_shape=pltpu.VMEM(right_side.shape, F32),
             in_specs=[pl.BlockSpec(memory_space=pl.ANY)] * 3
             + [pl.BlockSpec(memory_space=pltpu.SMEM)],
             out_specs=pl.BlockSpec(memory_space=pltpu.VMEM),
             scratch_shapes=[
                 big, big, pltpu.VMEM((8, 32, 256), jnp.int32), big, big, big, big, big,
+                big, two, two,
                 pltpu.VMEM((8, 32, 256), F32),
-                pltpu.VMEM((4, 32, 256), F32), pltpu.VMEM((6, 32, 256), F32),
-                pltpu.VMEM((4, 32, 256), F32), pltpu.VMEM((6, 32, 256), F32),
-                pltpu.VMEM((6, 32, 256), F32),
+                pltpu.VMEM((4, 32, 256), F32), coarse, coarse, coarse, coarse2, coarse2,
+                coarse, coarse,
                 pltpu.VMEM((2, 8, 8, 256), F32), pltpu.VMEM((2, 8, 8, 256), F32),
                 pltpu.VMEM((4, 2, 8, 256), F32),
+                pltpu.VMEM((2, 8, 8, 256), F32), pltpu.VMEM((4, 8, 256), F32),
                 msg, pltpu.VMEM((n1 - 1, 4, 128), F32),
                 msg, pltpu.VMEM((ny - 1, 4, 128), F32),
                 msg, pltpu.VMEM((nz - 1, 4, 128), F32),

time: 50.8 us -> 48.1 us (0.947)
  Pallas kernels: 48.9 us -> 47.3 us
  local copies, waits for them, and re-layouts: 1.67 us -> 0.71 us
    pallas_call x1, Pallas kernels: 48.9 us -> 47.3 us  [body(): pl.pallas_call(make_kernel(n_down, n_cross, nz), out_shape=pltpu.VMEM(rig...]
    unnamed x1, local copies, waits for them, and re-layouts: 1.67 us -> 0.71 us
where the time goes in v2:
time: 48.1 us; the launch traced here: 48 us
  Pallas kernels  47.3 us (98%)
  local copies, waits for them, and re-layouts  0.71 us (1%)
    pallas_call x1, Pallas kernels, body(): pl.pallas_call(make_kernel(n_down, n_cross, nz), out_shape=pltpu.VMEM(rig...  47.3 us

profile of v2, /device:TPU:1, one launch (start us, length us, event | category | flops | bytes accessed | tf_op | source)
XLA Modules:
  0.0 48.0 jit_solution(10442354660252434258)
XLA Ops:
  0.0 47.3 %cycle.1 = f32[8,32,256]{2,1,0:T(8,128)S(1)} custom-call(f32[8,32,256]{2,1,0:T(8,128)} %rhs_hbm.1, f32[8,32,256]{2,1,0:T(8,128)} %kappa_hbm.1, s32[8,32,256]{2,1,0:T(8,128)} %mask_hbm.1, s32[1,4]{1,0:T(1,128)} %route.1), custom_call_target="tpu_custom_call" | custom-call | tf_op jit(solution)/shard_map/cycle/pallas_call | solution.py:467
  47.3 0.7 %copy.6 = f32[8,32,256]{2,1,0:T(8,128)} copy(f32[8,32,256]{2,1,0:T(8,128)S(1)} %cycle.1) | data formatting | bytes 524288

commit v3 on v2

--- a/solution.py
+++ b/solution.py
@@ -67,7 +67,7 @@
         E, R, MK, D, W, PA, PB, Q, FX, FY, FZ, RES, CR, CC, WT, TX, TY, TZ, FA, FB,
         SX, LX, LK, QX, QK, M1, G1, M2, G2, M3, G3,
         load_sem, h_send, h_recv, q_send, q_recv,
-        s1, r1, s2, r2, s3, r3,
+        s1, r1, s2, r2, s3, r3, chain,
     ):
         d = lax.axis_index("down")
         c = lax.axis_index("cross")
@@ -100,7 +100,15 @@
         group3 = [((y * nz + lax.rem(z + k, nz)) * 2 + core, c) for k in range(1, nz)]
 
         barrier = pltpu.get_barrier_semaphore()
-        peers = near + corners + group1 + group2 + group3
+        def at_z(by):
+            return ((y * nz + lax.rem(z + nz + by, nz)) * 2 + core, c)
+
+        def at_y(by):
+            return ((lax.rem(y + ny + by, ny) * nz + z) * 2 + core, c)
+
+        beside = [at_z(1), at_z(-1), at_y(1), at_y(-1)]
+        rounds = [beside, [at_z(2), at_z(-2), at_y(2), at_y(-2)], [at_z(2), at_z(-2)]]
+        peers = near + corners + group1 + beside
         for peer in peers:
             pl.semaphore_signal(barrier, inc=1, device_id=peer, device_id_type=MESH)
 
@@ -127,6 +135,13 @@
             SX[1, x] = jnp.where(sub8 >= 5, E[x + 3, 24:32, :], pltpu.roll(R[x + 3, 24:32, :], 5, 0))
 
         pl.semaphore_wait(barrier, len(peers))
+
+        def announce(k):
+            for peer in rounds[k]:
+                pl.semaphore_signal(chain.at[k], inc=1, device_id=peer, device_id_type=MESH)
+
+        def heard(k):
+            pl.semaphore_wait(chain.at[k], len(rounds[k]))
 
         def remote(src, dst, send, recv, k, peer):
             return pltpu.make_async_remote_copy(
@@ -148,8 +163,11 @@
             halo.append(remote(src, LK.at[3 - k], h_send, h_recv, 6 + k, corners[k]))
         for k in (6, 7, 8, 9, 0, 1, 2, 3, 4, 5):
             halo[k].start()
+        announce(0)
         for copy in halo:
             copy.wait_recv()
+        heard(0)
+        announce(1)
 
         def unpack(left, right, i, keep):
             right, left = right * (m_r * keep), left * (m_l * keep)
@@ -193,6 +211,9 @@
             W[i] = w
             PA[i] = w * R[i]
 
+        heard(1)
+        announce(2)
+
         def coupling(p, i, n):
             back, ahead_, below, above = rolled(p[i], 1, n)
             along = FX[i, :n] * p[i - 1, :n] + FX[i + 1, :n] * p[i + 1, :n]
@@ -326,6 +347,7 @@
         for k in range(ny - 1):
             row = row + G2[k]
         M3[...] = row
+        heard(2)
         for copy in gather3:
             copy.start()
         for copy in fix_halo:
@@ -484,7 +506,7 @@
                 msg, pltpu.VMEM((nz - 1, 4, 128), F32),
                 dma((3,)), dma((10,)), dma((10,)), dma((8,)), dma((8,)),
                 dma((n1 - 1,)), dma((n1 - 1,)), dma((ny - 1,)), dma((ny - 1,)),
-                dma((nz - 1,)), dma((nz - 1,)),
+                dma((nz - 1,)), dma((nz - 1,)), pltpu.SemaphoreType.REGULAR((3,)),
             ],
             compiler_params=pltpu.CompilerParams(collective_id=0, has_side_effects=True),
             name="cycle",

time: 48.1 us -> 46.9 us (0.975)
  Pallas kernels: 47.3 us -> 46 us
    pallas_call x1, Pallas kernels: 47.3 us -> 46 us  [body(): pl.pallas_call(make_kernel(n_down, n_cross, nz), out_shape=pltpu.VMEM(rig...]
where the time goes in v3:
time: 46.9 us; the launch traced here: 46.7 us
  Pallas kernels  46 us (98%)
  local copies, waits for them, and re-layouts  0.71 us (2%)
    pallas_call x1, Pallas kernels, body(): pl.pallas_call(make_kernel(n_down, n_cross, nz), out_shape=pltpu.VMEM(rig...  46 us

profile of v3, /device:TPU:1, one launch (start us, length us, event | category | flops | bytes accessed | tf_op | source)
XLA Modules:
  0.0 46.7 jit_solution(9574393101188006967)
XLA Ops:
  0.0 46.0 %cycle.1 = f32[8,32,256]{2,1,0:T(8,128)S(1)} custom-call(f32[8,32,256]{2,1,0:T(8,128)} %rhs_hbm.1, f32[8,32,256]{2,1,0:T(8,128)} %kappa_hbm.1, s32[8,32,256]{2,1,0:T(8,128)} %mask_hbm.1, s32[1,4]{1,0:T(1,128)} %route.1), custom_call_target="tpu_custom_call" | custom-call | tf_op jit(solution)/shard_map/cycle/pallas_call | solution.py:489
  46.0 0.7 %copy.6 = f32[8,32,256]{2,1,0:T(8,128)} copy(f32[8,32,256]{2,1,0:T(8,128)S(1)} %cycle.1) | data formatting | bytes 524288

commit v4 on v3

--- a/solution.py
+++ b/solution.py
@@ -65,7 +65,7 @@
     def kernel(
         rhs_hbm, kappa_hbm, mask_hbm, route, out,
         E, R, MK, D, W, PA, PB, Q, FX, FY, FZ, RES, CR, CC, WT, TX, TY, TZ, FA, FB,
-        SX, LX, LK, QX, QK, M1, G1, M2, G2, M3, G3,
+        SX, LX, LK, QX, QK, U, V, GA, GS, GD, GC, M1, G1, M2, G2, M3, G3,
         load_sem, h_send, h_recv, q_send, q_recv,
         s1, r1, s2, r2, s3, r3, chain,
     ):
@@ -166,8 +166,6 @@
         announce(0)
         for copy in halo:
             copy.wait_recv()
-        heard(0)
-        announce(1)
 
         def unpack(left, right, i, keep):
             right, left = right * (m_r * keep), left * (m_l * keep)
@@ -211,14 +209,17 @@
             W[i] = w
             PA[i] = w * R[i]
 
-        heard(1)
-        announce(2)
+        heard(0)
+        announce(1)
 
         def coupling(p, i, n):
             back, ahead_, below, above = rolled(p[i], 1, n)
             along = FX[i, :n] * p[i - 1, :n] + FX[i + 1, :n] * p[i + 1, :n]
             across = FY[0, i, :n] * back + FY[1, i, :n] * ahead_
             return (along + across) + (FZ[0, i, :n] * below + FZ[1, i, :n] * above)
+
+        def spread(p, i, n):
+            return (1.0 - OMEGA) * p[i, :n] + W[i, :n] * coupling(p, i, n)
 
         def relax(p, i, n):
             return (1.0 - OMEGA) * p[i, :n] + W[i, :n] * (R[i, :n] + coupling(p, i, n))
@@ -258,6 +259,8 @@
         gather3 = [remote(M3, G3.at[k], s3, r3, k, group3[k]) for k in range(nz - 1)]
         for copy in gather1:
             copy.start()
+        heard(1)
+        announce(2)
 
         zero32 = jnp.zeros((32, 256), F32)
         for ref in (CC, FA, FB):
@@ -341,6 +344,42 @@
         for copy in fix_halo:
             copy.start()
 
+        zero32 = jnp.zeros((32, 256), F32)
+        zero40 = jnp.zeros((40, 256), F32)
+        side = jnp.where(sub8 < 4, m_r, m_l) + zero8
+
+        def ones(i, band_value, tile_value):
+            U[i, 0:32, :] = zero32 + band_value
+            U[i, 32:40, :] = side * tile_value
+
+        def set_ones(inner, inner_side, outer, outer_side):
+            for i, keep in ((1, m_up), (2, m_up), (11, m_dn), (12, m_dn)):
+                ones(i, outer * keep, outer_side * keep)
+
+            @pl.loop(3, 11)
+            def _(i):
+                ones(i, inner, inner_side)
+
+        for target, inner, outer in ((GA, 1.0, 1.0), (GS, 0.0, 0.0)):
+            set_ones(inner, 1.0, outer, outer)
+
+            @pl.loop(2, 12)
+            def _(i):
+                V[i] = spread(U, i, 40)
+
+            @pl.loop(3, 11)
+            def _(i, target=target):
+                target[i - 3] = spread(V, i, 32)
+
+        for i in (4, 5, 8, 9):
+            V[i] = zero40
+        for target, outer, rows in ((GD, 1.0, (3, 4, 9, 10)), (GC, 0.0, (3, 10))):
+            set_ones(0.0, 0.0, outer, 1.0 - outer)
+            for i in (2, 3, 10, 11):
+                V[i] = spread(U, i, 40)
+            for k, i in enumerate(rows):
+                target[k] = spread(V, i, 32)
+
         for copy in gather2:
             copy.wait_recv()
         row = M2[...]
@@ -352,6 +391,32 @@
             copy.start()
         for copy in fix_halo:
             copy.wait_recv()
+
+        for lo, hi, keep in ((1, 3, m_up), (3, 11, 1.0), (11, 13, m_dn)):
+
+            @pl.loop(lo, hi)
+            def _(i, keep=keep):
+                PA[i, 0:32, :] = Q[i, 0:32, :] * keep
+
+        def beside_tile(left, right, keep):
+            return jnp.where(sub8 < 4, right * m_r, left * m_l) * keep
+
+        @pl.loop(0, 8)
+        def _(x):
+            PA[x + 3, 32:40, :] = beside_tile(QX[0, x], QX[1, x], 1.0)
+
+        PA[1, 32:40, :] = zero8
+        PA[2, 32:40, :] = beside_tile(QK[0], QK[1], m_up)
+        PA[11, 32:40, :] = beside_tile(QK[2], QK[3], m_dn)
+        PA[12, 32:40, :] = zero8
+
+        @pl.loop(2, 12)
+        def _(i):
+            PB[i] = relax(PA, i, 40)
+
+        @pl.loop(3, 11)
+        def _(i):
+            out[i - 3] = relax(PB, i, 32)
 
         sub, lane = iota((8, 128), 0), iota((8, 128), 1)
         tz = 2 * sub + lane // 64
@@ -417,16 +482,20 @@
             return image
 
         def iterate(step, carry):
-            answer, resid, search, norm_now = carry
-            image = operate(search)
-            alpha = norm_now / total_of(search * image)
+            answer, resid, search, image, over_norm, over_alpha = carry
+            shown = operate(resid)
+            norm = total_of(resid * resid)
+            weight = total_of(resid * shown)
+            beta = norm * over_norm
+            alpha = norm / (weight - beta * (norm * over_alpha))
+            search = resid + beta * search
+            image = shown + beta * image
             answer = answer + alpha * search
             resid = resid - alpha * image
-            norm_next = total_of(resid * resid)
-            search = resid + norm_next / norm_now * search
-            return answer, resid, search, norm_next
-
-        start = (jnp.zeros((8, 128), F32), totals, totals, total_of(totals * totals))
+            return answer, resid, search, image, 1.0 / norm, 1.0 / alpha
+
+        none, nil = jnp.zeros((8, 128), F32), jnp.zeros((1, 1), F32)
+        start = (none, totals, none, none, nil, nil)
         answer = lax.fori_loop(0, COARSE_ITERS, iterate, start)[0]
 
         def brick(dd, cc):
@@ -435,37 +504,20 @@
             at_lane = lax.rem(z_b, 2) * 64 + y_b * 8 + cc * 2 + core_b
             return total_of(jnp.where((sub == lax.div(z_b, 2)) & (lane == at_lane), answer, 0.0))
 
-        for dd, lo, hi, keep in ((d_prev, 1, 3, m_up), (d, 3, 11, 1.0), (d_next, 11, 13, m_dn)):
-            left, own_, right = brick(dd, c_prev), brick(dd, c), brick(dd, c_next)
-
-            @pl.loop(lo, hi)
-            def _(i, own_=own_, keep=keep):
-                PA[i, 0:32, :] = (Q[i, 0:32, :] + own_) * keep
-
-            def beside(side_l, side_r, left=left, right=right, keep=keep):
-                tile = jnp.where(sub8 < 4, (side_r + right) * m_r, (side_l + left) * m_l)
-                return tile * keep
-
-            if lo == 3:
-
-                @pl.loop(0, 8)
-                def _(x, beside=beside):
-                    PA[x + 3, 32:40, :] = beside(QX[0, x], QX[1, x])
-
-            elif lo == 1:
-                PA[1, 32:40, :] = zero8
-                PA[2, 32:40, :] = beside(QK[0], QK[1])
-            else:
-                PA[11, 32:40, :] = beside(QK[2], QK[3])
-                PA[12, 32:40, :] = zero8
-
-        @pl.loop(2, 12)
-        def _(i):
-            PB[i] = relax(PA, i, 40)
-
-        @pl.loop(3, 11)
-        def _(i):
-            out[i - 3] = relax(PB, i, 32)
+        mine = brick(d, c)
+        near_by = [brick(dd, cc) - mine for dd, cc in near]
+        at_corner = [brick(dd, cc) - mine for dd, cc in corners]
+        first_half = iota((32, 256), 0) < 16
+        beside_by = jnp.where(first_half, near_by[2], near_by[3])
+
+        @pl.loop(0, 8)
+        def _(x):
+            out[x] = out[x] + (mine * GA[x] + beside_by * GS[x])
+
+        for k, x in enumerate((0, 1, 6, 7)):
+            out[x] = out[x] + near_by[k // 2] * GD[k]
+        for k, x in enumerate((0, 7)):
+            out[x] = out[x] + jnp.where(first_half, at_corner[2 * k], at_corner[2 * k + 1]) * GC[k]
 
         for copy in halo + gather1 + gather2 + gather3 + fix_halo:
             copy.wait_send()
@@ -501,6 +553,8 @@
                 pltpu.VMEM((2, 8, 8, 256), F32), pltpu.VMEM((2, 8, 8, 256), F32),
                 pltpu.VMEM((4, 2, 8, 256), F32),
                 pltpu.VMEM((2, 8, 8, 256), F32), pltpu.VMEM((4, 8, 256), F32),
+                big, big, pltpu.VMEM((8, 32, 256), F32), pltpu.VMEM((8, 32, 256), F32),
+                pltpu.VMEM((4, 32, 256), F32), pltpu.VMEM((2, 32, 256), F32),
                 msg, pltpu.VMEM((n1 - 1, 4, 128), F32),
                 msg, pltpu.VMEM((ny - 1, 4, 128), F32),
                 msg, pltpu.VMEM((nz - 1, 4, 128), F32),

time: 46.9 us -> 42.9 us (0.915)
  Pallas kernels: 46 us -> 42 us
    pallas_call x1, Pallas kernels: 46 us -> 42 us  [body(): pl.pallas_call(make_kernel(n_down, n_cross, nz), out_shape=pltpu.VMEM(rig...]
where the time goes in v4:
time: 42.9 us; the launch traced here: 42.7 us
  Pallas kernels  42 us (98%)
  local copies, waits for them, and re-layouts  0.71 us (2%)
    pallas_call x1, Pallas kernels, body(): pl.pallas_call(make_kernel(n_down, n_cross, nz), out_shape=pltpu.VMEM(rig...  42 us

profile of v4, /device:TPU:1, one launch (start us, length us, event | category | flops | bytes accessed | tf_op | source)
XLA Modules:
  0.0 42.7 jit_solution(4819329258963469774)
XLA Ops:
  0.0 42.0 %cycle.1 = f32[8,32,256]{2,1,0:T(8,128)S(1)} custom-call(f32[8,32,256]{2,1,0:T(8,128)} %rhs_hbm.1, f32[8,32,256]{2,1,0:T(8,128)} %kappa_hbm.1, s32[8,32,256]{2,1,0:T(8,128)} %mask_hbm.1, s32[1,4]{1,0:T(1,128)} %route.1), custom_call_target="tpu_custom_call" | custom-call | tf_op jit(solution)/shard_map/cycle/pallas_call | solution.py:541
  42.0 0.7 %copy.6 = f32[8,32,256]{2,1,0:T(8,128)} copy(f32[8,32,256]{2,1,0:T(8,128)S(1)} %cycle.1) | data formatting | bytes 524288

commit v5 on v4

--- a/solution.py
+++ b/solution.py
@@ -161,11 +161,27 @@
             rows = slice(0, 2) if sx < 0 else slice(6, 8)
             src = SX.at[0 if sy < 0 else 1, rows]
             halo.append(remote(src, LK.at[3 - k], h_send, h_recv, 6 + k, corners[k]))
-        for k in (6, 7, 8, 9, 0, 1, 2, 3, 4, 5):
+        for k in (0, 1, 2, 3, 6, 7, 8, 9, 4, 5):
             halo[k].start()
         announce(0)
-        for copy in halo:
-            copy.wait_recv()
+
+        lane32 = iota((32, 256), 1)
+
+        @pl.loop(3, 11)
+        def _(i):
+            q = E[i, 0:32, :]
+            below = jnp.where(lane32 > 0, pltpu.roll(q, 1, 1), 0.0)
+            above = jnp.where(lane32 < 255, pltpu.roll(q, 255, 1), 0.0)
+            FZ[0, i, 0:32, :] = jnp.where(lane32 > 0, 0.5 * (below + q), 0.0)
+            FZ[1, i, 0:32, :] = jnp.where(lane32 < 255, 0.5 * (above + q), 0.0)
+            D[i, 0:32, :] = 3.0 * q + 0.5 * (below + above)
+
+        @pl.loop(4, 11)
+        def _(i):
+            FX[i, 0:32, :] = 0.5 * (E[i - 1, 0:32, :] + E[i, 0:32, :])
+
+        for k in (0, 1, 2, 3, 6, 7, 8, 9):
+            halo[k].wait_recv()
 
         def unpack(left, right, i, keep):
             right, left = right * (m_r * keep), left * (m_l * keep)
@@ -181,33 +197,64 @@
         def _(x):
             unpack(LK[0, x], LK[1, x], x + 1, m_up)
             unpack(LK[2, x], LK[3, x], x + 11, m_dn)
+
+        @pl.loop(0, 3)
+        def _(x):
+            E[x, 0:32, :] = E[x, 0:32, :] * m_up
+            E[x + 11, 0:32, :] = E[x + 11, 0:32, :] * m_dn
+
+        lane40, lane8 = iota((40, 256), 1), iota((8, 256), 1)
+
+        def weigh(q, diag):
+            inside = q > 0
+            return jnp.where(inside, OMEGA / jnp.where(inside, diag, 1.0), 0.0)
+
+        @pl.loop(3, 11)
+        def _(i):
+            q, up, dn = E[i], E[i - 1], E[i + 1]
+            back, ahead_ = pltpu.roll(q, 1, 0), pltpu.roll(q, 39, 0)
+            FY[0, i] = 0.5 * (back + q)
+            FY[1, i] = 0.5 * (ahead_ + q)
+            around = 0.5 * ((up + dn) + (back + ahead_))
+            g = q[32:40]
+            below = jnp.where(lane8 > 0, pltpu.roll(g, 1, 1), 0.0)
+            above = jnp.where(lane8 < 255, pltpu.roll(g, 255, 1), 0.0)
+            FZ[0, i, 32:40, :] = jnp.where(lane8 > 0, 0.5 * (below + g), 0.0)
+            FZ[1, i, 32:40, :] = jnp.where(lane8 < 255, 0.5 * (above + g), 0.0)
+            FX[i, 32:40, :] = 0.5 * (up[32:40] + g)
+            diag = D[i, 0:32, :] + around[0:32]
+            diag_g = 3.0 * g + 0.5 * (below + above) + around[32:40]
+            w, w_g = weigh(q[0:32], diag), weigh(g, diag_g)
+            D[i, 0:32, :] = diag
+            W[i, 0:32, :] = w
+            W[i, 32:40, :] = w_g
+            PA[i, 0:32, :] = w * R[i, 0:32, :]
+            PA[i, 32:40, :] = w_g * R[i, 32:40, :]
+
+        for k in (4, 5):
+            halo[k].wait_recv()
+
+        @pl.loop(0, 2)
+        def _(x):
             R[x + 1, 0:32, :] = R[x + 1, 0:32, :] * m_up
             R[x + 11, 0:32, :] = R[x + 11, 0:32, :] * m_dn
 
-        @pl.loop(0, 3)
-        def _(x):
-            E[x, 0:32, :] = E[x, 0:32, :] * m_up
-            E[x + 11, 0:32, :] = E[x + 11, 0:32, :] * m_dn
-
-        lane40 = iota((40, 256), 1)
-
-        @pl.loop(1, 13)
-        def _(i):
+        @pl.loop(0, 4)
+        def _(x):
+            i = x + 1 + 8 * lax.div(x, 2)
             q = E[i]
             back, ahead_, below, above = shifted(q, 1)
             up, dn = E[i - 1], E[i + 1]
-            diag = 3.0 * q + 0.5 * (((up + dn) + (back + ahead_)) + (below + above))
-            inside = q > 0
-            w = jnp.where(inside, OMEGA / jnp.where(inside, diag, 1.0), 0.0)
             FX[i] = 0.5 * (up + q)
-            FX[i + 1] = 0.5 * (dn + q)
             FY[0, i] = 0.5 * (back + q)
             FY[1, i] = 0.5 * (ahead_ + q)
             FZ[0, i] = jnp.where(lane40 > 0, 0.5 * (below + q), 0.0)
             FZ[1, i] = jnp.where(lane40 < 255, 0.5 * (above + q), 0.0)
-            D[i] = diag
+            w = weigh(q, 3.0 * q + 0.5 * (((up + dn) + (back + ahead_)) + (below + above)))
             W[i] = w
             PA[i] = w * R[i]
+
+        FX[3, 0:32, :] = 0.5 * (E[2, 0:32, :] + E[3, 0:32, :])
 
         heard(0)
         announce(1)
@@ -257,8 +304,13 @@
         gather1 = [remote(M1, G1.at[k], s1, r1, k, group1[k]) for k in range(n1 - 1)]
         gather2 = [remote(M2, G2.at[k], s2, r2, k, group2[k]) for k in range(ny - 1)]
         gather3 = [remote(M3, G3.at[k], s3, r3, k, group3[k]) for k in range(nz - 1)]
-        for copy in gather1:
-            copy.start()
+
+        def launch(copies):
+            middle = (len(copies) - 1) / 2
+            for k in sorted(range(len(copies)), key=lambda k: abs(k - middle)):
+                copies[k].start()
+
+        launch(gather1)
         heard(1)
         announce(2)
 
@@ -272,7 +324,7 @@
             CR[x] = pair_sum(RES[2 * x] + RES[2 * x + 1])
             CC[x + 1] = 0.125 * pair_sum(E[2 * x + 3, 0:32, :] + E[2 * x + 4, 0:32, :])
 
-        lane32, row32 = iota((32, 256), 1), iota((32, 256), 0) % 8
+        row32 = iota((32, 256), 0) % 8
 
         @pl.loop(1, 5)
         def _(i):
@@ -324,8 +376,7 @@
         for k in range(n1 - 1):
             row = row + G1[k]
         M2[...] = row
-        for copy in gather2:
-            copy.start()
+        launch(gather2)
 
         src_rows = {-1: slice(3, 5), 1: slice(9, 11)}
         dst_rows = {-1: slice(11, 13), 1: slice(1, 3)}
@@ -387,8 +438,7 @@
             row = row + G2[k]
         M3[...] = row
         heard(2)
-        for copy in gather3:
-            copy.start()
+        launch(gather3)
         for copy in fix_halo:
             copy.wait_recv()
 
@@ -424,6 +474,8 @@
         tc = (lane % 8) // 2
         odd = lane % 2 == 1
 
+        for copy in halo + gather1 + gather2 + fix_halo + gather3:
+            copy.wait_send()
         for copy in gather3:
             copy.wait_recv()
         table = [jnp.where(sub == lax.div(z, 2), M3[k : k + 1, :], 0.0) for k in range(4)]
@@ -519,8 +571,6 @@
         for k, x in enumerate((0, 7)):
             out[x] = out[x] + jnp.where(first_half, at_corner[2 * k], at_corner[2 * k + 1]) * GC[k]
 
-        for copy in halo + gather1 + gather2 + gather3 + fix_halo:
-            copy.wait_send()
 
     return kernel
 

time: 42.9 us -> 42.3 us (0.986)
  Pallas kernels: 42 us -> 41.1 us
    pallas_call x1, Pallas kernels: 42 us -> 41.1 us  [body(): pl.pallas_call(make_kernel(n_down, n_cross, nz), out_shape=pltpu.VMEM(rig...]
where the time goes in v5:
time: 42.3 us; the launch traced here: 41.9 us
  Pallas kernels  41.1 us (97%)
  local copies, waits for them, and re-layouts  0.71 us (2%)
    pallas_call x1, Pallas kernels, body(): pl.pallas_call(make_kernel(n_down, n_cross, nz), out_shape=pltpu.VMEM(rig...  41.1 us

profile of v5, /device:TPU:1, one launch (start us, length us, event | category | flops | bytes accessed | tf_op | source)
XLA Modules:
  0.0 41.9 jit_solution(4384217628667148651)
XLA Ops:
  0.0 41.1 %cycle.1 = f32[8,32,256]{2,1,0:T(8,128)S(1)} custom-call(f32[8,32,256]{2,1,0:T(8,128)} %rhs_hbm.1, f32[8,32,256]{2,1,0:T(8,128)} %kappa_hbm.1, s32[8,32,256]{2,1,0:T(8,128)} %mask_hbm.1, s32[1,4]{1,0:T(1,128)} %route.1), custom_call_target="tpu_custom_call" | custom-call | tf_op jit(solution)/shard_map/cycle/pallas_call | solution.py:591
  41.1 0.7 %copy.6 = f32[8,32,256]{2,1,0:T(8,128)} copy(f32[8,32,256]{2,1,0:T(8,128)S(1)} %cycle.1) | data formatting | bytes 524288

commit v6 on v5

--- a/solution.py
+++ b/solution.py
@@ -65,7 +65,7 @@
     def kernel(
         rhs_hbm, kappa_hbm, mask_hbm, route, out,
         E, R, MK, D, W, PA, PB, Q, FX, FY, FZ, RES, CR, CC, WT, TX, TY, TZ, FA, FB,
-        SX, LX, LK, QX, QK, U, V, GA, GS, GD, GC, M1, G1, M2, G2, M3, G3,
+        SX, LX, LK, QX, QK, U, V, S, GA, GS, GD, GC, M1, G1, M2, G2, M3, G3,
         load_sem, h_send, h_recv, q_send, q_recv,
         s1, r1, s2, r2, s3, r3, chain,
     ):
@@ -126,13 +126,7 @@
             kap = E[x + 3, 0:32, :]
             E[x + 3, 0:32, :] = jnp.where(MK[x] > 0, kap * 0.25, kap)
 
-        loads[2].wait()
         sub8 = iota((8, 256), 0)
-
-        @pl.loop(0, 8)
-        def _(x):
-            SX[0, x] = jnp.where(sub8 < 3, E[x + 3, 0:8, :], pltpu.roll(R[x + 3, 0:8, :], 3, 0))
-            SX[1, x] = jnp.where(sub8 >= 5, E[x + 3, 24:32, :], pltpu.roll(R[x + 3, 24:32, :], 5, 0))
 
         pl.semaphore_wait(barrier, len(peers))
 
@@ -161,7 +155,16 @@
             rows = slice(0, 2) if sx < 0 else slice(6, 8)
             src = SX.at[0 if sy < 0 else 1, rows]
             halo.append(remote(src, LK.at[3 - k], h_send, h_recv, 6 + k, corners[k]))
-        for k in (0, 1, 2, 3, 6, 7, 8, 9, 4, 5):
+        halo[0].start()
+        halo[1].start()
+        loads[2].wait()
+
+        @pl.loop(0, 8)
+        def _(x):
+            SX[0, x] = jnp.where(sub8 < 3, E[x + 3, 0:8, :], pltpu.roll(R[x + 3, 0:8, :], 3, 0))
+            SX[1, x] = jnp.where(sub8 >= 5, E[x + 3, 24:32, :], pltpu.roll(R[x + 3, 24:32, :], 5, 0))
+
+        for k in (2, 3, 6, 7, 8, 9, 4, 5):
             halo[k].start()
         announce(0)
 
@@ -180,6 +183,11 @@
         def _(i):
             FX[i, 0:32, :] = 0.5 * (E[i - 1, 0:32, :] + E[i, 0:32, :])
 
+        sourced = lax.fori_loop(3, 11, lambda i, acc: acc + R[i, 0:32, :], jnp.zeros((32, 256), F32))
+        sourced = sourced[0:8] + sourced[8:16] + sourced[16:24] + sourced[24:32]
+
+        heard(0)
+        announce(1)
         for k in (0, 1, 2, 3, 6, 7, 8, 9):
             halo[k].wait_recv()
 
@@ -256,8 +264,6 @@
 
         FX[3, 0:32, :] = 0.5 * (E[2, 0:32, :] + E[3, 0:32, :])
 
-        heard(0)
-        announce(1)
 
         def coupling(p, i, n):
             back, ahead_, below, above = rolled(p[i], 1, n)
@@ -265,6 +271,12 @@
             across = FY[0, i, :n] * back + FY[1, i, :n] * ahead_
             return (along + across) + (FZ[0, i, :n] * below + FZ[1, i, :n] * above)
 
+        def spread_flat(p, i):
+            v = p[i]
+            along = FX[i] * p[i - 1] + FX[i + 1] * p[i + 1]
+            across = FY[0, i] * pltpu.roll(v, 1, 0) + FY[1, i] * pltpu.roll(v, 39, 0)
+            return (1.0 - OMEGA) * v + W[i] * ((along + across) + (FZ[0, i] + FZ[1, i]) * v)
+
         def spread(p, i, n):
             return (1.0 - OMEGA) * p[i, :n] + W[i, :n] * coupling(p, i, n)
 
@@ -275,16 +287,23 @@
         def _(i):
             PB[i] = relax(PA, i, 40)
 
-        def residual_row(x, carry):
+        left = FX[3, 0:32, :] * (PB[3, 0:32, :] - PB[2, 0:32, :])
+        left = left + FX[11, 0:32, :] * (PB[10, 0:32, :] - PB[11, 0:32, :])
+        left = left[0:8] + left[8:16] + left[16:24] + left[24:32]
+
+        def faces(i, carry):
             acc, con = carry
-            i = x + 3
-            res = R[i, :32] - D[i, :32] * PB[i, :32] + coupling(PB, i, 32)
-            RES[x] = res
-            return acc + res, con + E[i]
-
-        acc, con = lax.fori_loop(
-            0, 8, residual_row, (jnp.zeros((32, 256), F32), jnp.zeros((40, 256), F32))
-        )
+            p, q, tile = PB[i, 0:32, :], E[i, 0:32, :], PB[i, 32:40, :]
+            end = (0.5 * q) * p
+            end = end[0:8] + end[8:16] + end[16:24] + end[24:32]
+            acc = acc + jnp.where((lane8 == 0) | (lane8 == 255), end, 0.0)
+            low = FY[0, i, 0:8, :] * (p[0:8] - pltpu.roll(tile, 1, 0))
+            high = FY[1, i, 24:32, :] * (p[24:32] - pltpu.roll(tile, 7, 0))
+            acc = acc + jnp.where(sub8 == 0, low, 0.0) + jnp.where(sub8 == 7, high, 0.0)
+            return acc, con + E[i]
+
+        left, con = lax.fori_loop(3, 11, faces, (left, jnp.zeros((40, 256), F32)))
+        acc = sourced - left
 
         sub40 = iota((40, 256), 0)
         own = sub40 < 32
@@ -311,8 +330,11 @@
                 copies[k].start()
 
         launch(gather1)
-        heard(1)
-        announce(2)
+
+        @pl.loop(0, 8)
+        def _(x):
+            i = x + 3
+            RES[x] = R[i, :32] - D[i, :32] * PB[i, :32] + coupling(PB, i, 32)
 
         zero32 = jnp.zeros((32, 256), F32)
         for ref in (CC, FA, FB):
@@ -370,6 +392,8 @@
             Q[2 * x + 3, 0:32, :] = PB[2 * x + 3, 0:32, :] + fix
             Q[2 * x + 4, 0:32, :] = PB[2 * x + 4, 0:32, :] + fix
 
+        heard(1)
+        announce(2)
         for copy in gather1:
             copy.wait_recv()
         row = M1[...]
@@ -411,23 +435,49 @@
             def _(i):
                 ones(i, inner, inner_side)
 
-        for target, inner, outer in ((GA, 1.0, 1.0), (GS, 0.0, 0.0)):
-            set_ones(inner, 1.0, outer, outer)
-
-            @pl.loop(2, 12)
-            def _(i):
-                V[i] = spread(U, i, 40)
-
-            @pl.loop(3, 11)
-            def _(i, target=target):
-                target[i - 3] = spread(V, i, 32)
+        set_ones(1.0, 1.0, 1.0, 1.0)
+
+        @pl.loop(2, 12)
+        def _(i):
+            V[i] = spread_flat(U, i)
+
+        @pl.loop(3, 11)
+        def _(i):
+            GA[i - 3] = spread(V, i, 32)
+
+        def cut(ref, *at):
+            return jnp.concatenate([ref[(*at, slice(24, 40))], ref[(*at, slice(0, 8))]], axis=0)
+
+        beside_one = jnp.concatenate([zero8, side, zero8], axis=0)
+        for i in (2, 11):
+            S[i] = jnp.zeros((24, 256), F32)
+
+        @pl.loop(3, 11)
+        def _(i):
+            along = cut(FX, i) * flag(i > 3) + cut(FX, i + 1) * flag(i < 10)
+            column = cut(FZ, 0, i) + cut(FZ, 1, i)
+            back, ahead_ = pltpu.roll(beside_one, 1, 0), pltpu.roll(beside_one, 23, 0)
+            across = cut(FY, 0, i) * back + cut(FY, 1, i) * ahead_
+            total = (along + column) * beside_one + across
+            S[i] = (1.0 - OMEGA) * beside_one + cut(W, i) * total
+
+        @pl.loop(3, 11)
+        def _(i):
+            v = S[i]
+            back, ahead_, below, above = rolled(v, 1, 24)
+            along = cut(FX, i) * S[i - 1] + cut(FX, i + 1) * S[i + 1]
+            across = cut(FY, 0, i) * back + cut(FY, 1, i) * ahead_
+            column = cut(FZ, 0, i) * below + cut(FZ, 1, i) * above
+            v = (1.0 - OMEGA) * v + cut(W, i) * ((along + across) + column)
+            GS[i - 3, 0:8, :] = v[16:24]
+            GS[i - 3, 8:16, :] = v[0:8]
 
         for i in (4, 5, 8, 9):
             V[i] = zero40
         for target, outer, rows in ((GD, 1.0, (3, 4, 9, 10)), (GC, 0.0, (3, 10))):
             set_ones(0.0, 0.0, outer, 1.0 - outer)
             for i in (2, 3, 10, 11):
-                V[i] = spread(U, i, 40)
+                V[i] = spread_flat(U, i)
             for k, i in enumerate(rows):
                 target[k] = spread(V, i, 32)
 
@@ -476,12 +526,11 @@
 
         for copy in halo + gather1 + gather2 + fix_halo + gather3:
             copy.wait_send()
-        for copy in gather3:
-            copy.wait_recv()
         table = [jnp.where(sub == lax.div(z, 2), M3[k : k + 1, :], 0.0) for k in range(4)]
-        for j in range(nz - 1):
+        for j in sorted(range(nz - 1), key=lambda j: -abs(j - (nz - 2) / 2)):
             from_z = lax.rem(z + nz - 1 - j, nz)
             at = sub == lax.div(from_z, 2)
+            gather3[j].wait_recv()
             for k in range(4):
                 table[k] = table[k] + jnp.where(at, G3[j, k : k + 1, :], 0.0)
         totals, outs, link_dn, link_cr = table
@@ -560,11 +609,13 @@
         near_by = [brick(dd, cc) - mine for dd, cc in near]
         at_corner = [brick(dd, cc) - mine for dd, cc in corners]
         first_half = iota((32, 256), 0) < 16
-        beside_by = jnp.where(first_half, near_by[2], near_by[3])
 
         @pl.loop(0, 8)
         def _(x):
-            out[x] = out[x] + (mine * GA[x] + beside_by * GS[x])
+            out[x, 8:24, :] = out[x, 8:24, :] + mine * GA[x, 8:24, :]
+            low, high = out[x, 0:8, :], out[x, 24:32, :]
+            out[x, 0:8, :] = low + (mine * GA[x, 0:8, :] + near_by[2] * GS[x, 0:8, :])
+            out[x, 24:32, :] = high + (mine * GA[x, 24:32, :] + near_by[3] * GS[x, 8:16, :])
 
         for k, x in enumerate((0, 1, 6, 7)):
             out[x] = out[x] + near_by[k // 2] * GD[k]
@@ -603,7 +654,8 @@
                 pltpu.VMEM((2, 8, 8, 256), F32), pltpu.VMEM((2, 8, 8, 256), F32),
                 pltpu.VMEM((4, 2, 8, 256), F32),
                 pltpu.VMEM((2, 8, 8, 256), F32), pltpu.VMEM((4, 8, 256), F32),
-                big, big, pltpu.VMEM((8, 32, 256), F32), pltpu.VMEM((8, 32, 256), F32),
+                big, big, pltpu.VMEM((14, 24, 256), F32),
+                pltpu.VMEM((8, 32, 256), F32), pltpu.VMEM((8, 16, 256), F32),
                 pltpu.VMEM((4, 32, 256), F32), pltpu.VMEM((2, 32, 256), F32),
                 msg, pltpu.VMEM((n1 - 1, 4, 128), F32),
                 msg, pltpu.VMEM((ny - 1, 4, 128), F32),

time: 42.3 us -> 41.7 us (0.986)
  Pallas kernels: 41.1 us -> 40.5 us
    pallas_call x1, Pallas kernels: 41.1 us -> 40.5 us  [body(): pl.pallas_call(make_kernel(n_down, n_cross, nz), out_shape=pltpu.VMEM(rig...]
where the time goes in v6:
time: 41.7 us; the launch traced here: 41.2 us
  Pallas kernels  40.5 us (97%)
  local copies, waits for them, and re-layouts  0.71 us (2%)
    pallas_call x1, Pallas kernels, body(): pl.pallas_call(make_kernel(n_down, n_cross, nz), out_shape=pltpu.VMEM(rig...  40.5 us

profile of v6, /device:TPU:1, one launch (start us, length us, event | category | flops | bytes accessed | tf_op | source)
XLA Modules:
  0.0 41.2 jit_solution(11607081901529162297)
XLA Ops:
  0.0 40.5 %cycle.1 = f32[8,32,256]{2,1,0:T(8,128)S(1)} custom-call(f32[8,32,256]{2,1,0:T(8,128)} %rhs_hbm.1, f32[8,32,256]{2,1,0:T(8,128)} %kappa_hbm.1, s32[8,32,256]{2,1,0:T(8,128)} %mask_hbm.1, s32[1,4]{1,0:T(1,128)} %route.1), custom_call_target="tpu_custom_call" | custom-call | tf_op jit(solution)/shard_map/cycle/pallas_call | solution.py:642
  40.5 0.7 %copy.6 = f32[8,32,256]{2,1,0:T(8,128)} copy(f32[8,32,256]{2,1,0:T(8,128)S(1)} %cycle.1) | data formatting | bytes 524288

commit v7 on v6

--- a/solution.py
+++ b/solution.py
@@ -472,6 +472,14 @@
             GS[i - 3, 0:8, :] = v[16:24]
             GS[i - 3, 8:16, :] = v[0:8]
 
+        for copy in gather2:
+            copy.wait_recv()
+        row = M2[...]
+        for k in range(ny - 1):
+            row = row + G2[k]
+        M3[...] = row
+        heard(2)
+        launch(gather3)
         for i in (4, 5, 8, 9):
             V[i] = zero40
         for target, outer, rows in ((GD, 1.0, (3, 4, 9, 10)), (GC, 0.0, (3, 10))):
@@ -480,15 +488,6 @@
                 V[i] = spread_flat(U, i)
             for k, i in enumerate(rows):
                 target[k] = spread(V, i, 32)
-
-        for copy in gather2:
-            copy.wait_recv()
-        row = M2[...]
-        for k in range(ny - 1):
-            row = row + G2[k]
-        M3[...] = row
-        heard(2)
-        launch(gather3)
         for copy in fix_halo:
             copy.wait_recv()
 

time: 41.7 us -> 41.7 us (level)
  no operation moved by 1% of the time
where the time goes in v7:
time: 41.7 us; the launch traced here: 41.2 us
  Pallas kernels  40.5 us (97%)
  local copies, waits for them, and re-layouts  0.71 us (2%)
    pallas_call x1, Pallas kernels, body(): pl.pallas_call(make_kernel(n_down, n_cross, nz), out_shape=pltpu.VMEM(rig...  40.5 us

profile of v7, /device:TPU:1, one launch (start us, length us, event | category | flops | bytes accessed | tf_op | source)
XLA Modules:
  0.0 41.2 jit_solution(2674407305240751500)
XLA Ops:
  0.0 40.5 %cycle.1 = f32[8,32,256]{2,1,0:T(8,128)S(1)} custom-call(f32[8,32,256]{2,1,0:T(8,128)} %rhs_hbm.1, f32[8,32,256]{2,1,0:T(8,128)} %kappa_hbm.1, s32[8,32,256]{2,1,0:T(8,128)} %mask_hbm.1, s32[1,4]{1,0:T(1,128)} %route.1), custom_call_target="tpu_custom_call" | custom-call | tf_op jit(solution)/shard_map/cycle/pallas_call | solution.py:641
  40.5 0.7 %copy.6 = f32[8,32,256]{2,1,0:T(8,128)} copy(f32[8,32,256]{2,1,0:T(8,128)S(1)} %cycle.1) | data formatting | bytes 524288
